TPU v7x, 1024 devices: a whole 8x8x8 slice. The times are simulated.
1024 devices in a mesh: rows: 16 (over z, core), cols: 64 (over x, y).
Axes of the slice: x: 8, y: 8, z: 8, core: 2. Of those that a mesh axis runs over, the one named last changes fastest.
Arguments:
- momentum_prev: float32 [8192, 8192], P('rows', 'cols'), may hold values from -170 to 170
- gradient: bfloat16 [8192, 8192], P('rows', 'cols'), may hold values from -6 to 6
- q_prev: float32 [8192, 512], P('cols'), may hold values from -0.0625 to 0.0625
Outputs:
- momentum_next: float32 [8192, 8192], P('rows', 'cols')
- q_next: float32 [8192, 512], P('cols')
- update: bfloat16 [8192, 8192], P('rows', 'cols')
All inputs are finite; a program needn't handle non-finite values.
Results may differ from a plain program's by a relative error of at most 0.001.
Values sent between devices are 32-bit elements; how exact they have to be, the bound alone decides.
A program may use at most 32 MiB of HBM per device.

v0:
```python
import jax
import jax.numpy as jnp
from jax import lax
from jax.sharding import PartitionSpec as P

D = 8192
RANK = 512


def body(momentum_prev, gradient, q_prev):
    highest = lax.Precision.HIGHEST
    momentum = 0.95 * momentum_prev + gradient.astype(jnp.float32)
    power_part = lax.psum_scatter(
        jnp.dot(momentum, q_prev, precision=highest, preferred_element_type=jnp.float32),
        "cols",
        scatter_dimension=0,
        tiled=True,
    )
    partial_gram = jnp.dot(
        power_part.T, power_part, precision=highest, preferred_element_type=jnp.float32
    )
    gram = lax.psum(partial_gram, ("rows", "cols"))
    chol = jnp.linalg.cholesky(gram)
    basis_part = lax.linalg.triangular_solve(
        chol, power_part, left_side=False, lower=True, transpose_a=True
    )
    basis = lax.all_gather(basis_part, "cols", axis=0, tiled=True)
    cross_part = lax.dot_general(
        momentum,
        basis,
        (((0,), (0,)), ((), ())),
        precision=highest,
        preferred_element_type=jnp.float32,
    )
    cross = lax.psum(cross_part, "rows")
    col_sq = lax.psum(jnp.sum(cross * cross, axis=0), "cols")
    q_next = cross / (jnp.sqrt(col_sq) + 1e-08)
    momentum_next = momentum - 0.5 * lax.dot_general(
        basis,
        cross,
        (((1,), (1,)), ((), ())),
        precision=highest,
        preferred_element_type=jnp.float32,
    )
    factor = D / jnp.sqrt(jnp.float32(RANK))
    update = (
        factor
        * lax.dot_general(
            basis,
            q_next,
            (((1,), (1,)), ((), ())),
            precision=highest,
            preferred_element_type=jnp.float32,
        )
    ).astype(jnp.bfloat16)
    return (momentum_next, q_next, update)


def solution(mesh):
    in_specs = (P("rows", "cols"), P("rows", "cols"), P("cols", None))
    out_specs = (P("rows", "cols"), P("cols", None), P("rows", "cols"))
    return jax.shard_map(body, mesh=mesh, in_specs=in_specs, out_specs=out_specs, check_vma=False)
```

profile of v0, /device:TPU:8, one launch (start us, length us, event | category | flops | bytes accessed | tf_op | source)
XLA Modules:
  0.0 989.6 jit_solution(15407318369314543805)
XLA Ops:
  7.2 0.0 copy-start
  7.2 0.0 all-reduce.10.cloned.1.call-start
  7.2 0.9 copy-done
  8.1 3.0 fusion.12
  11.2 0.0 all-reduce.10.cloned.1.call-update
  11.2 0.0 all-reduce.6.cloned.1.call-start
  11.2 1.3 dynamic-slice.3
  13.2 180.3 %all-reduce.10.cloned.1.call-done = f32[512,512]{1,0:T(8,128)} async-done(((f32[512,512]{1,0:T(8,128)}), f32[512,512]{1,0:T(8,128)}) %all-reduce.10.cloned.1.call-update) | async-done | bytes 1048592
  193.5 2.8 fusion.23
  196.3 0.0 all-reduce.6.cloned.1.call-update
  196.3 0.0 all-gather.2.cloned.1.call-start
  196.4 291.8 %all-reduce.6.cloned.1.call-done = f32[512,512]{0,1:T(8,128)} async-done(((f32[512,512]{0,1:T(8,128)}), f32[512,512]{0,1:T(8,128)}) %all-reduce.6.cloned.1.call-update) | async-done | bytes 1048592 | tf_op jit(solution)/shard_map/psum | solution.py:22
  488.2 1.6 copy.9
  489.9 0.2 fusion.2
  490.1 11.7 %cholesky.104 = f32[128,128]{1,0:T(8,128)S(1)} custom-call(f32[128,128]{1,0:T(8,128)S(1)} %cholesky.266), custom_call_target="Cholesky" | custom-call | tf_op jit(solution)/shard_map/jit(cholesky)/cholesky | solution.py:23
  501.9 9.8 custom-call.30
  511.7 0.1 cholesky.224
  511.8 0.3 constant_dynamic-update-slice_fusion.3
  512.1 0.3 convolution_subtract_fusion
  512.5 11.7 %cholesky.217 = f32[128,128]{1,0:T(8,128)S(1)} custom-call(f32[128,128]{1,0:T(8,128)S(1)} %cholesky.270), custom_call_target="Cholesky" | custom-call | tf_op jit(solution)/shard_map/jit(cholesky)/cholesky | solution.py:23
  524.2 10.0 %custom-call.31 = f32[1,128,128]{1,2,0:T(8,128)S(1)} custom-call(f32[1,128,128]{2,1,0:T(8,128)S(1)} %get-tuple-element.27), custom_call_target="InvertDiagBlocksLowerTriangular" | custom-call | tf_op jit(solution)/shard_map/jit(cholesky)/cholesky | solution.py:23
  534.2 0.3 convolution_dynamic-update-slice_fusion
  534.5 0.4 convolution_subtract_fusion.1
  534.9 11.7 %cholesky.238 = f32[128,128]{1,0:T(8,128)S(1)} custom-call(f32[128,128]{1,0:T(8,128)S(1)} %cholesky.275), custom_call_target="Cholesky" | custom-call | tf_op jit(solution)/shard_map/jit(cholesky)/cholesky | solution.py:23
  546.6 0.7 compare_reduce_fusion.1
  547.3 9.8 custom-call.32
  557.1 0.2 convolution_dynamic-update-slice_fusion.1
  557.3 0.4 convolution_subtract_fusion.2
  557.7 11.7 %cholesky.255 = f32[128,128]{1,0:T(8,128)S(1)} custom-call(f32[128,128]{1,0:T(8,128)S(1)} %convolution_subtract_fusion.2), custom_call_target="Cholesky" | custom-call | tf_op jit(solution)/shard_map/jit(cholesky)/cholesky | solution.py:23
  569.5 0.6 compare_reduce_fusion
  570.1 0.7 compare_reduce_fusion.2
  573.3 0.3 select_select_fusion
  573.7 10.9 %while.1 = (s32[]{:T(128)}, f32[512,512]{1,0:T(8,128)S(1)}, s32[4,2]{0,1:T(2,128)S(1)}, f32[4,128,128]{2,1,0:T(8,128)}, s32[]{:T(128)}) while((s32[]{:T(128)}, f32[512,512]{1,0:T(8,128)S(1)}, s32[4,2]{0,1:T(2,128)S(1)}, f32[4,128,128]{2,1,0:T(8,128)}, s32[]{:T(128)}) %tuple.31), condition=%wide.while_cond, body=%wide.while_body.sunk | while | flops 2 | bytes 132705 | solution.py:24
  573.7 0.1 constant_dynamic-slice_fusion.2
  573.8 0.6 fusion.53
  574.4 2.1 bitcast_dynamic-update-slice_fusion.2
  576.4 0.1 constant_dynamic-slice_fusion.2
  576.5 0.6 fusion.53
  577.1 2.1 bitcast_dynamic-update-slice_fusion.2
  579.2 0.1 constant_dynamic-slice_fusion.2
  579.2 0.6 fusion.53
  579.8 2.1 bitcast_dynamic-update-slice_fusion.2
  581.9 0.1 constant_dynamic-slice_fusion.2
  582.0 0.6 fusion.53
  582.6 2.1 bitcast_dynamic-update-slice_fusion.2
  584.6 40.1 %custom-call.33 = f32[4,128,128]{1,2,0:T(8,128)S(1)} custom-call(f32[4,128,128]{2,1,0:T(8,128)} %get-tuple-element.10), custom_call_target="InvertDiagBlocksLowerTriangular" | custom-call | tf_op jit(solution)/shard_map/triangular_solve | solution.py:24
  624.7 0.8 fusion.17
  625.6 0.9 convolution_subtract_fusion.5
  626.5 0.2 fusion.15
  626.7 0.9 convolution_subtract_fusion.4
  627.6 0.2 fusion.14
  627.8 1.0 convolution_subtract_fusion.3
  628.8 0.2 fusion.13
  629.0 0.6 pad_maximum_fusion
  629.7 0.0 all-gather.2.cloned.1.call-update
  629.7 0.0 all-reduce.8.cloned.1.call-start
  629.7 82.0 %all-gather.2.cloned.1.call-done = f32[512,512]{1,0:T(8,128)} async-done(((f32[8,512]{1,0:T(8,128)}), f32[512,512]{1,0:T(8,128)}) %all-gather.2.cloned.1.call-update) | async-done | bytes 1048592 | tf_op jit(solution)/shard_map/all_gather | solution.py:27
  711.8 2.8 fusion.11
  714.6 0.0 all-reduce.8.cloned.1.call-update
  714.6 123.0 %all-reduce.8.cloned.1.call-done = f32[128,512]{1,0:T(8,128)} async-done(((f32[128,512]{1,0:T(8,128)}), f32[128,512]{1,0:T(8,128)}) %all-reduce.8.cloned.1.call-update) | async-done | bytes 262160 | tf_op jit(solution)/shard_map/psum | solution.py:35
  837.6 1.1 multiply_reduce_fusion
  838.7 140.9 %psum.23 = f32[512]{0:T(512)S(1)} all-reduce(f32[512]{0:T(512)S(1)} %multiply_reduce_fusion), channel_id=1, replica_groups=mesh['rows'=16,'cols'=64] {'cols'}, use_global_device_ids=true, to_apply=%region_12.13 | all-reduce | flops 512 | bytes 4096 | tf_op jit(solution)/shard_map/psum | solution.py:36
  979.6 1.7 fusion
  981.4 1.6 fusion.1
  (24 shorter events, 0.2 us)
Async XLA Ops:
  7.2 1.0 copy-start
  7.2 186.3 %all-reduce.10.cloned.1.call-start = ((), (), s32[]{:S(2)}) async-start(), calls=%async_computation.3 | async-start | bytes 2097152
  11.2 477.0 %all-reduce.6.cloned.1.call-start = ((), (), s32[]{:S(2)}) async-start(), calls=%async_computation | async-start | bytes 2097152 | tf_op jit(solution)/shard_map/psum | solution.py:22
  196.3 515.5 %all-gather.2.cloned.1.call-start = ((), (), s32[]{:S(2)}) async-start(), calls=%async_computation.1 | async-start | bytes 1064960 | tf_op jit(solution)/shard_map/all_gather | solution.py:27
  488.2 1.7 copy-start.2
  626.7 85.1 %copy-start.4 = (f32[512,128]{1,0:T(8,128)S(1)}, f32[512,128]{1,0:T(8,128)}, u32[]{:S(2)}) copy-start(f32[512,128]{1,0:T(8,128)} %param.3) | copy-start | bytes 786436
  627.8 84.0 %copy-start.5 = (bf16[512,128]{1,0:T(8,128)(2,1)S(1)}, bf16[512,128]{1,0:T(8,128)(2,1)}, u32[]{:S(2)}) copy-start(bf16[512,128]{1,0:T(8,128)(2,1)} %param.4) | copy-start | bytes 393220
  629.7 208.0 %all-reduce.8.cloned.1.call-start = ((), (), s32[]{:S(2)}) async-start(), calls=%async_computation.2 | async-start | bytes 524288 | tf_op jit(solution)/shard_map/psum | solution.py:35
  711.8 267.9 %copy-start.1 = (f32[512,512]{1,0:T(8,128)S(1)}, f32[512,512]{1,0:T(8,128)}, u32[]{:S(2)}) copy-start(f32[512,512]{1,0:T(8,128)} %all-gather.2.cloned.1.call-done) | copy-start | bytes 3145732
  837.6 142.0 %copy-start.3 = (f32[128,512]{1,0:T(8,128)S(1)}, f32[128,512]{1,0:T(8,128)}, u32[]{:S(2)}) copy-start(f32[128,512]{1,0:T(8,128)} %all-reduce.8.cloned.1.call-done) | copy-start | bytes 786436
  981.4 1.7 copy-start.6
Sparse Core Ops, SparseCore 0:
  11.3 182.1 all-reduce.9
  198.2 289.9 all-reduce.5
  629.8 81.9 all-gather.1
  714.7 122.8 all-reduce.7
where the time goes:
time: 990 us
  waiting for transfers between devices  677 us (68%)
  blocking collectives  141 us (14%)
  other arithmetic  121 us (12%)
  matrix products  18.1 us (2%)
  between operations  17.2 us (2%)
  local copies, waits for them, and re-layouts  14.9 us (2%)
    psum x1, waiting for transfers between devices, body(): gram = lax.psum(partial_gram, ('rows', 'cols'))  292 us
    unnamed x5, waiting for transfers between devices  180 us
    psum x1, blocking collectives, body(): col_sq = lax.psum(jnp.sum(cross * cross, axis=0), 'cols')  141 us
    psum x1, waiting for transfers between devices, body(): cross = lax.psum(cross_part, 'rows')  123 us
    all_gather x1, waiting for transfers between devices, body(): basis = lax.all_gather(basis_part, 'cols', axis=0, tiled=True)  82 us
    another operation x14, other arithmetic, body(): chol = jnp.linalg.cholesky(gram)  78.6 us
    another operation x4, other arithmetic, body(): lax.linalg.triangular_solve(chol, power_part, left_side=False, lower=True...  41.1 us
  transfers between devices with their start and end apart: 4, of which 4 were waited for; matrix products, arithmetic and copies ran while one was open for 0% of the time, Pallas kernels for 0%

commit v1 on v0

v1 whole, which is shorter than its diff:
```python
import functools

import jax
import jax.numpy as jnp
from jax import lax
from jax.experimental import pallas as pl
from jax.experimental.pallas import tpu as pltpu
from jax.sharding import PartitionSpec as P

D = 8192
RANK = 512
HALF = RANK // 2
MESH = pl.DeviceIdType.MESH
VMEM = pltpu.VMEM
F32 = jnp.float32
HIGH = lax.Precision.HIGH


def order(n):
    return sorted(range(1, n), key=lambda d: -min(d, n - d))


class Grid:
    def __init__(self, nx, ny, nz):
        self.n = (nx, ny)
        self.nz = nz
        self.r = lax.axis_index("rows")
        self.c = lax.axis_index("cols")
        self.at = (lax.div(self.c, ny), lax.rem(self.c, ny))
        self.z, self.core = lax.div(self.r, 2), lax.rem(self.r, 2)

    def along(self, axis, d):
        return lax.rem(self.at[axis] + d, self.n[axis])

    def peer(self, axis, d):
        place = [self.at[0], self.at[1]]
        place[axis] = self.along(axis, d)
        return (self.r, place[0] * self.n[1] + place[1])

    def z_along(self, d):
        return lax.rem(self.z + d, self.nz)

    def z_peer(self, d):
        return (self.z_along(d) * 2 + self.core, self.c)

    def sibling(self):
        return (self.r + 1 - 2 * self.core, self.c)

    def plane_peers(self):
        return [self.peer(a, d) for a in (0, 1) for d in range(1, self.n[a])]

    def row_peers(self):
        return [self.sibling()] + [self.z_peer(d) for d in range(1, self.nz)]


def enter(peers):
    barrier = pltpu.get_barrier_semaphore()
    for device in peers:
        pl.semaphore_signal(barrier, inc=1, device_id=device, device_id_type=MESH)
    pl.semaphore_wait(barrier, len(peers))


def send(src, dst, sems, slot, device):
    copy = pltpu.make_async_remote_copy(
        src_ref=src,
        dst_ref=dst,
        send_sem=sems.at[(0,) + slot],
        recv_sem=sems.at[(1,) + slot],
        device_id=device,
        device_id_type=MESH,
    )
    copy.start()
    return copy


def power_kernel(nx, ny, nz, part, out, recv1, sum1, recv2, gather, sem1, sem2, sem3, sem4):
    g = Grid(nx, ny, nz)
    enter(g.plane_peers())
    rows = part.shape[0]
    big = [rows // g.n[h] for h in (0, 1)]
    small = [big[h] // g.n[1 - h] for h in (0, 1)]
    columns = [pl.ds(h * HALF, HALF) for h in (0, 1)]
    sent = []

    def block(i, size):
        return pl.ds(pl.multiple_of(i * size, size), size)

    first = [[], []]
    for h in (0, 1):
        for d in order(g.n[h]):
            first[h].append(
                send(
                    part.at[block(g.along(h, d), big[h]), columns[h]],
                    recv1.at[h, d - 1],
                    sem1,
                    (h, d - 1),
                    g.peer(h, d),
                )
            )
    second = [[], []]
    for h in (0, 1):
        total = part[block(g.at[h], big[h]), columns[h]]
        for copy in first[h]:
            copy.wait_recv()
        for d in range(1, g.n[h]):
            total = total + recv1[h, d - 1]
        sum1[h] = total
        for d in order(g.n[1 - h]):
            second[h].append(
                send(
                    sum1.at[h, block(g.along(1 - h, d), small[h])],
                    recv2.at[h, d - 1],
                    sem2,
                    (h, d - 1),
                    g.peer(1 - h, d),
                )
            )
    third = [[], []]
    for h in (0, 1):
        mine = block(g.at[1 - h], small[h])
        total = sum1[h, mine]
        for copy in second[h]:
            copy.wait_recv()
        for d in range(1, g.n[1 - h]):
            total = total + recv2[h, d - 1]
        gather[h, mine] = total
        for d in order(g.n[1 - h]):
            third[h].append(
                send(gather.at[h, mine], gather.at[h, mine], sem3, (h, d - 1), g.peer(1 - h, d))
            )
    fourth = [[], []]
    for h in (0, 1):
        for copy in third[h]:
            copy.wait_recv()
        mine = block(g.at[h], big[h])
        for d in order(g.n[h]):
            fourth[h].append(
                send(gather.at[h], out.at[mine, columns[h]], sem4, (h, d - 1), g.peer(h, d))
            )
        out[mine, columns[h]] = gather[h]
    for stage in (first, second, third, fourth):
        for h in (0, 1):
            for copy in stage[h]:
                copy.wait_send()
    for h in (0, 1):
        for copy in fourth[h]:
            copy.wait_recv()


def power_sum(nx, ny, nz, part):
    rows = part.shape[0]
    big, small = rows // nx, rows // nx // ny
    return pl.pallas_call(
        functools.partial(power_kernel, nx, ny, nz),
        name="power_sum",
        out_shape=jax.ShapeDtypeStruct((rows, RANK), F32),
        in_specs=[pl.BlockSpec(memory_space=VMEM)],
        out_specs=pl.BlockSpec(memory_space=VMEM),
        scratch_shapes=[
            VMEM((2, nx - 1, big, HALF), F32),
            VMEM((2, big, HALF), F32),
            VMEM((2, ny - 1, small, HALF), F32),
            VMEM((2, big, HALF), F32),
        ]
        + [pltpu.SemaphoreType.DMA((2, 2, nx - 1))] * 4,
        compiler_params=pltpu.CompilerParams(collective_id=0, has_side_effects=True),
    )(part)


def gram_kernel(
    nx, ny, nz, gram, cross, whole, crossed,
    gram_core, gram_z, cross_core, cross_sum, cross_z,
    core_sem, z_sem, plane_sem, back_sem,
):
    g = Grid(nx, ny, nz)
    enter(g.plane_peers() + g.row_peers())
    core, other = g.core, 1 - g.core
    x, y = g.at
    share = cross.shape[1] // nz

    def block(i):
        return pl.ds(pl.multiple_of(i * share, share), share)

    swap = [
        send(gram.at[other], gram_core, core_sem, (0,), g.sibling()),
        send(cross.at[other], cross_core, core_sem, (1,), g.sibling()),
    ]
    swap[0].wait_recv()
    gram_z[g.z] = gram[core] + gram_core[...]
    ups = []
    for d in order(nz):
        ups.append(send(gram_z.at[g.z], gram_z.at[g.z], z_sem, (0, d - 1), g.z_peer(d)))
    swap[1].wait_recv()
    cross_sum[...] = cross[core] + cross_core[...]
    shares = []
    for d in order(nz):
        shares.append(
            send(cross_sum.at[block(g.z_along(d))], cross_z.at[d - 1], z_sem, (1, d - 1), g.z_peer(d))
        )
    for copy in ups:
        copy.wait_recv()
    total = gram_z[0]
    for i in range(1, nz):
        total = total + gram_z[i]
    width = HALF // 2
    near = [[], []]
    for q in (0, 1):
        place = whole.at[core * 2 + q, x, y]
        whole[core * 2 + q, x, y] = total[:, q * width : (q + 1) * width]
        for d in order(g.n[1 - q]):
            near[q].append(send(place, place, plane_sem, (0, q, d - 1), g.peer(1 - q, d)))
    for copy in shares:
        copy.wait_recv()
    mine = block(g.z)
    total = cross_sum[mine]
    for d in range(1, nz):
        total = total + cross_z[d - 1]
    crossed[core, mine] = total
    gathers = []
    for d in order(nz):
        gathers.append(
            send(crossed.at[core, mine], crossed.at[core, mine], z_sem, (2, d - 1), g.z_peer(d))
        )
    far = [[], []]
    for q in (0, 1):
        for copy in near[q]:
            copy.wait_recv()
        place = whole.at[core * 2 + q, x] if q == 0 else whole.at[core * 2 + q, :, y]
        for d in order(g.n[q]):
            far[q].append(send(place, place, plane_sem, (1, q, d - 1), g.peer(q, d)))
    for copy in gathers:
        copy.wait_recv()
    back = [send(crossed.at[core], crossed.at[core], back_sem, (0,), g.sibling())]
    for q in (0, 1):
        for copy in far[q]:
            copy.wait_recv()
        place = whole.at[core * 2 + q]
        back.append(send(place, place, back_sem, (1 + q,), g.sibling()))
    for copy in swap + ups + shares + gathers + near[0] + near[1] + far[0] + far[1]:
        copy.wait_send()
    for copy in back:
        copy.wait()


def gram_sum(nx, ny, nz, gram, cross):
    rows, depth = gram.shape[1], cross.shape[1]
    return pl.pallas_call(
        functools.partial(gram_kernel, nx, ny, nz),
        name="gram_sum",
        out_shape=(
            jax.ShapeDtypeStruct((4, nx, ny, rows, HALF // 2), F32),
            jax.ShapeDtypeStruct((2, depth, HALF), F32),
        ),
        in_specs=[pl.BlockSpec(memory_space=VMEM)] * 2,
        out_specs=(pl.BlockSpec(memory_space=VMEM),) * 2,
        scratch_shapes=[
            VMEM((rows, HALF), F32),
            VMEM((nz, rows, HALF), F32),
            VMEM((depth, HALF), F32),
            VMEM((depth, HALF), F32),
            VMEM((nz - 1, depth // nz, HALF), F32),
            pltpu.SemaphoreType.DMA((2, 2)),
            pltpu.SemaphoreType.DMA((2, 3, nz - 1)),
            pltpu.SemaphoreType.DMA((2, 2, 2, nx - 1)),
            pltpu.SemaphoreType.DMA((2, 3)),
        ],
        compiler_params=pltpu.CompilerParams(collective_id=1, has_side_effects=True),
    )(gram, cross)


def norm_kernel(nx, ny, nz, part, out, recv, total, sems):
    g = Grid(nx, ny, nz)
    enter(g.plane_peers())
    copies = []
    total[...] = part[...]
    for axis in (0, 1):
        here = []
        for d in order(g.n[axis]):
            here.append(
                send(total.at[axis], recv.at[axis, d - 1], sems, (axis, d - 1), g.peer(axis, d))
            )
        for copy in here:
            copy.wait_recv()
        value = total[axis]
        for d in range(1, g.n[axis]):
            value = value + recv[axis, d - 1]
        if axis == 0:
            total[1] = value
        else:
            out[...] = value
        copies += here
    for copy in copies:
        copy.wait_send()


def norm_sum(nx, ny, nz, part):
    return pl.pallas_call(
        functools.partial(norm_kernel, nx, ny, nz),
        name="norm_sum",
        out_shape=jax.ShapeDtypeStruct((1, RANK), F32),
        in_specs=[pl.BlockSpec(memory_space=VMEM)],
        out_specs=pl.BlockSpec(memory_space=VMEM),
        scratch_shapes=[
            VMEM((2, nx - 1, 1, RANK), F32),
            VMEM((2, 1, RANK), F32),
            pltpu.SemaphoreType.DMA((2, 2, nx - 1)),
        ],
        compiler_params=pltpu.CompilerParams(collective_id=2, has_side_effects=True),
    )(jnp.broadcast_to(part, (2, 1, RANK)))


def dot(a, b, ca, cb):
    return lax.dot_general(
        a, b, (((ca,), (cb,)), ((), ())), precision=HIGH, preferred_element_type=F32
    )


def inverse_factor(gram):
    chol = jnp.linalg.cholesky(gram, symmetrize_input=False)
    return lax.linalg.triangular_solve(
        chol, jnp.eye(RANK, dtype=F32), left_side=True, lower=True
    )


def body(nx, ny, nz, momentum_prev, gradient, q_prev):
    momentum = 0.95 * momentum_prev + gradient.astype(F32)
    power = power_sum(nx, ny, nz, dot(momentum, q_prev, 1, 0))
    rows = RANK // (nx * ny)
    mine = lax.dynamic_slice(power, (0, rows * lax.axis_index("cols")), (power.shape[0], rows))
    gram_part = dot(mine, power, 0, 0).reshape(rows, 2, HALF).transpose(1, 0, 2)
    depth = momentum.shape[1]
    cross_part = dot(momentum, power, 0, 0).reshape(depth, 2, HALF).transpose(1, 0, 2)
    gram, crossed = gram_sum(nx, ny, nz, gram_part, cross_part)
    gram = gram.reshape(4, RANK, RANK // 4).transpose(1, 0, 2).reshape(RANK, RANK)
    crossed = crossed.transpose(1, 0, 2).reshape(depth, RANK)
    inverse = inverse_factor(gram)
    cross = dot(crossed, inverse, 1, 1)
    col_sq = norm_sum(nx, ny, nz, jnp.sum(cross * cross, axis=0, keepdims=True))
    q_next = cross / (jnp.sqrt(col_sq) + 1e-08)
    factor = D / jnp.sqrt(jnp.float32(RANK))
    both = jnp.concatenate([-0.5 * cross, factor * q_next], axis=0)
    product = dot(power, dot(inverse, both, 0, 1), 1, 0)
    return (
        momentum + product[:, :depth],
        q_next,
        product[:, depth:].astype(jnp.bfloat16),
    )


def sizes(mesh):
    side = {64: 8, 16: 4, 4: 2}[mesh.shape["cols"]]
    return side, side, mesh.shape["rows"] // 2


def solution(mesh):
    in_specs = (P("rows", "cols"), P("rows", "cols"), P("cols", None))
    out_specs = (P("rows", "cols"), P("cols", None), P("rows", "cols"))
    return jax.shard_map(
        functools.partial(body, *sizes(mesh)),
        mesh=mesh,
        in_specs=in_specs,
        out_specs=out_specs,
        check_vma=False,
    )
```

time: 990 us -> 270 us (0.27)
  the two profiles are of different devices: /device:TPU:8 before, /device:TPU:1 now
where the time goes in v1:
time: 270 us; the launch traced here: 269 us
  other arithmetic  131 us (49%)
  Pallas kernels  100 us (37%)
  local copies, waits for them, and re-layouts  18.6 us (7%)
  matrix products  15.8 us (6%)
  between operations  3.58 us (1%)
    another operation x14, other arithmetic, inverse_factor(): chol = jnp.linalg.cholesky(gram, symmetrize_input=False)  88.8 us
    pallas_call x1, Pallas kernels, gram_sum(): pl.pallas_call(functools.partial(gram_kernel, nx, ny, nz), name='gram_sum...  45.5 us
    pallas_call x1, Pallas kernels, power_sum(): pl.pallas_call(functools.partial(power_kernel, nx, ny, nz), name='power_s...  42.2 us
    another operation x3, other arithmetic, inverse_factor(): lax.linalg.triangular_solve(chol, jnp.eye(RANK, dtype=F32), left_side=Tru...  39.4 us
    pallas_call x1, Pallas kernels, norm_sum(): pl.pallas_call(functools.partial(norm_kernel, nx, ny, nz), name='norm_sum...  12.4 us
    dot_general x6, matrix products, dot(): lax.dot_general(a, b, (((ca,), (cb,)), ((), ())), precision=HIGH, preferr...  8.35 us
    another operation x12, local copies, waits for them, and re-layouts  7.92 us

profile of v1, /device:TPU:1, one launch (start us, length us, event | category | flops | bytes accessed | tf_op | source)
XLA Modules:
  0.0 268.9 jit_solution(7554670277933196924)
XLA Ops:
  0.6 0.9 copy-done
  1.6 2.6 fusion.27.part
  4.2 42.2 %power_sum.1 = f32[512,512]{1,0:T(8,128)} custom-call(f32[512,512]{1,0:T(8,128)} %fusion.27.part), custom_call_target="tpu_custom_call" | custom-call | tf_op jit(solution)/shard_map/power_sum/pallas_call | solution.py:153
  46.4 2.5 fusion.15
  48.9 1.0 fusion.26
  49.9 0.8 copy.8
  50.7 45.5 %gram_sum.1 = (f32[4,8,8,8,128]{4,3,2,1,0:T(8,128)}, f32[2,128,256]{2,1,0:T(8,128)}) custom-call(f32[2,8,256]{2,1,0:T(8,128)} %bitcast.75, f32[2,128,256]{2,1,0:T(8,128)} %bitcast.71), custom_call_target="tpu_custom_call" | custom-call | tf_op jit(solution)/shard_map/gram_sum/pallas_call | solution.py:247
  96.3 1.9 copy.9
  98.3 11.7 %cholesky.104 = f32[128,128]{1,0:T(8,128)S(1)} custom-call(f32[128,128]{1,0:T(8,128)S(1)} %cholesky.266), custom_call_target="Cholesky" | custom-call | tf_op jit(solution)/shard_map/jit(cholesky)/cholesky | solution.py:319
  110.0 0.6 copy-done.9
  110.6 10.4 %custom-call.30 = f32[1,128,128]{1,2,0:T(8,128)} custom-call(f32[1,128,128]{2,1,0:T(8,128)S(1)} %get-tuple-element.37), custom_call_target="InvertDiagBlocksLowerTriangular" | custom-call | tf_op jit(solution)/shard_map/jit(cholesky)/cholesky | solution.py:319
  121.1 1.0 cholesky.224
  122.1 0.3 constant_dynamic-update-slice_fusion.3
  122.4 0.3 convolution_subtract_fusion.3
  122.7 0.7 copy-done.5
  123.4 0.6 cholesky.270
  124.0 13.3 %cholesky.217 = f32[128,128]{1,0:T(8,128)} custom-call(f32[128,128]{1,0:T(8,128)} %cholesky.270), custom_call_target="Cholesky" | custom-call | tf_op jit(solution)/shard_map/jit(cholesky)/cholesky | solution.py:319
  137.4 1.5 select_reduce_fusion.2
  138.9 0.7 compare_reduce_fusion.2
  140.8 11.3 %custom-call.31 = f32[1,128,128]{1,2,0:T(8,128)} custom-call(f32[1,128,128]{2,1,0:T(8,128)} %get-tuple-element.34), custom_call_target="InvertDiagBlocksLowerTriangular" | custom-call | tf_op jit(solution)/shard_map/jit(cholesky)/cholesky | solution.py:319
  152.1 1.2 convolution_dynamic-update-slice_fusion
  153.3 0.4 convolution_subtract_fusion.4
  153.7 0.6 copy-done.6
  154.3 0.6 cholesky.275
  155.0 13.2 %cholesky.238 = f32[128,128]{1,0:T(8,128)} custom-call(f32[128,128]{1,0:T(8,128)} %cholesky.275), custom_call_target="Cholesky" | custom-call | tf_op jit(solution)/shard_map/jit(cholesky)/cholesky | solution.py:319
  168.1 1.5 select_reduce_fusion.1
  169.6 0.6 compare_reduce_fusion.1
  170.9 11.3 %custom-call.32 = f32[1,128,128]{1,2,0:T(8,128)} custom-call(f32[1,128,128]{2,1,0:T(8,128)} %get-tuple-element.31), custom_call_target="InvertDiagBlocksLowerTriangular" | custom-call | tf_op jit(solution)/shard_map/jit(cholesky)/cholesky | solution.py:319
  182.2 1.1 convolution_dynamic-update-slice_fusion.1
  183.3 1.2 convolution_subtract_fusion.5
  184.5 12.5 %cholesky.255 = f32[128,128]{1,0:T(8,128)S(1)} custom-call(f32[128,128]{1,0:T(8,128)} %convolution_subtract_fusion.5), custom_call_target="Cholesky" | custom-call | tf_op jit(solution)/shard_map/jit(cholesky)/cholesky | solution.py:319
  197.1 0.6 compare_reduce_fusion
  198.4 0.1 select_select_fusion
  198.6 8.0 %while.1 = (s32[]{:T(128)}, f32[512,512]{1,0:T(8,128)S(1)}, s32[4,2]{0,1:T(2,128)S(1)}, f32[4,128,128]{2,1,0:T(8,128)S(1)}, s32[]{:T(128)}) while((s32[]{:T(128)}, f32[512,512]{1,0:T(8,128)S(1)}, s32[4,2]{0,1:T(2,128)S(1)}, f32[4,128,128]{2,1,0:T(8,128)S(1)}, s32[]{:T(128)}) %tuple.34), condition=%wide.while_cond, body=%wide.while_body.sunk | while | flops 2 | bytes 131181 | solution.py:320
  198.6 0.5 fusion.58
  199.2 1.4 bitcast_dynamic-update-slice_fusion.2
  200.6 0.5 fusion.58
  201.2 1.4 bitcast_dynamic-update-slice_fusion.2
  202.6 0.5 fusion.58
  203.2 1.4 bitcast_dynamic-update-slice_fusion.2
  204.7 0.5 fusion.58
  205.2 1.4 bitcast_dynamic-update-slice_fusion.2
  206.6 39.3 %custom-call.33 = f32[4,128,128]{1,2,0:T(8,128)S(1)} custom-call(f32[4,128,128]{2,1,0:T(8,128)S(1)} %get-tuple-element.14), custom_call_target="InvertDiagBlocksLowerTriangular" | custom-call | tf_op jit(solution)/shard_map/triangular_solve | solution.py:320
  246.0 0.3 fusion.17
  246.3 0.1 fusion.13
  246.4 0.4 convolution_subtract_fusion.1
  246.8 0.4 fusion.31
  247.3 0.4 convolution_subtract_fusion
  247.7 0.5 copy-done.8
  248.2 0.4 fusion.29
  248.6 0.6 convolution_subtract_fusion.2
  249.3 0.4 fusion.28
  249.7 0.5 copy-done.10
  250.2 0.1 copy.10
  250.4 0.7 multiply_reduce_fusion
  251.1 0.6 broadcast_in_dim.6.part
  251.7 12.4 %norm_sum.1 = f32[1,512]{1,0:T(1,128)} custom-call(f32[2,1,512]{2,1,0:T(1,128)} %broadcast_in_dim.6.part), custom_call_target="tpu_custom_call" | custom-call | tf_op jit(solution)/shard_map/norm_sum/pallas_call | solution.py:297
  264.1 0.7 sqrt_add_fusion
  264.8 0.8 broadcast_multiply_fusion
  265.6 1.0 fusion.5
  266.6 0.6 fusion.45
  267.2 0.3 copy-done.3
  267.5 0.7 slice_add_fusion
  268.3 0.7 slice.127
  (29 shorter events, 0.6 us)
Async XLA Ops:
  0.6 1.0 copy-start
  4.2 44.7 %copy-start.2 = (f32[512,128]{1,0:T(8,128)S(1)}, f32[512,128]{1,0:T(8,128)}, u32[]{:S(2)}) copy-start(f32[512,128]{1,0:T(8,128)} %param.3) | copy-start | bytes 786436
  4.2 44.7 %copy-start.4 = (bf16[512,128]{1,0:T(8,128)(2,1)S(1)}, bf16[512,128]{1,0:T(8,128)(2,1)}, u32[]{:S(2)}) copy-start(bf16[512,128]{1,0:T(8,128)(2,1)} %param.4) | copy-start | bytes 393220
  46.4 2.5 copy-start.1
  110.0 0.6 copy-start.9
  121.1 1.0 copy-start.11
  122.7 0.7 copy-start.5
  153.7 0.7 copy-start.6
  245.9 0.9 copy-start.7
  247.3 1.0 copy-start.8
  249.3 1.0 copy-start.10
  266.6 1.0 copy-start.3

commit v2 on v1

--- a/solution.py
+++ b/solution.py
@@ -10,6 +10,7 @@
 D = 8192
 RANK = 512
 HALF = RANK // 2
+BLOCK = 128
 MESH = pl.DeviceIdType.MESH
 VMEM = pltpu.VMEM
 F32 = jnp.float32
@@ -71,6 +72,20 @@
     )
     copy.start()
     return copy
+
+
+def split(a):
+    high = a.astype(jnp.bfloat16)
+    return high, (a - high.astype(F32)).astype(jnp.bfloat16)
+
+
+def dot3(a, b, ca, cb):
+    (a_high, a_low), (b_high, b_low) = split(a), split(b)
+
+    def one(p, q):
+        return lax.dot_general(p, q, (((ca,), (cb,)), ((), ())), preferred_element_type=F32)
+
+    return one(a_high, b_high) + (one(a_high, b_low) + one(a_low, b_high))
 
 
 def power_kernel(nx, ny, nz, part, out, recv1, sum1, recv2, gather, sem1, sem2, sem3, sem4):
@@ -168,30 +183,31 @@
 
 
 def gram_kernel(
-    nx, ny, nz, gram, cross, whole, crossed,
-    gram_core, gram_z, cross_core, cross_sum, cross_z,
+    nx, ny, nz, gram, momentum, power, whole, crossed,
+    gram_core, gram_z, cross, cross_core, cross_sum, cross_z,
     core_sem, z_sem, plane_sem, back_sem,
 ):
     g = Grid(nx, ny, nz)
     enter(g.plane_peers() + g.row_peers())
-    core, other = g.core, 1 - g.core
+    core = g.core
     x, y = g.at
-    share = cross.shape[1] // nz
+    share = cross.shape[0] // nz
+    own = pl.ds(pl.multiple_of(core * HALF, HALF), HALF)
+    other = pl.ds(pl.multiple_of((1 - core) * HALF, HALF), HALF)
 
     def block(i):
         return pl.ds(pl.multiple_of(i * share, share), share)
 
-    swap = [
-        send(gram.at[other], gram_core, core_sem, (0,), g.sibling()),
-        send(cross.at[other], cross_core, core_sem, (1,), g.sibling()),
-    ]
+    swap = [send(gram.at[:, other], gram_core, core_sem, (0,), g.sibling())]
+    cross[...] = dot3(momentum[...], power[...], 0, 0)
+    swap.append(send(cross.at[:, other], cross_core, core_sem, (1,), g.sibling()))
     swap[0].wait_recv()
-    gram_z[g.z] = gram[core] + gram_core[...]
+    gram_z[g.z] = gram[:, own] + gram_core[...]
     ups = []
     for d in order(nz):
         ups.append(send(gram_z.at[g.z], gram_z.at[g.z], z_sem, (0, d - 1), g.z_peer(d)))
     swap[1].wait_recv()
-    cross_sum[...] = cross[core] + cross_core[...]
+    cross_sum[...] = cross[:, own] + cross_core[...]
     shares = []
     for d in order(nz):
         shares.append(
@@ -215,11 +231,11 @@
     total = cross_sum[mine]
     for d in range(1, nz):
         total = total + cross_z[d - 1]
-    crossed[core, mine] = total
+    crossed[mine, own] = total
     gathers = []
     for d in order(nz):
         gathers.append(
-            send(crossed.at[core, mine], crossed.at[core, mine], z_sem, (2, d - 1), g.z_peer(d))
+            send(crossed.at[mine, own], crossed.at[mine, own], z_sem, (2, d - 1), g.z_peer(d))
         )
     far = [[], []]
     for q in (0, 1):
@@ -230,7 +246,7 @@
             far[q].append(send(place, place, plane_sem, (1, q, d - 1), g.peer(q, d)))
     for copy in gathers:
         copy.wait_recv()
-    back = [send(crossed.at[core], crossed.at[core], back_sem, (0,), g.sibling())]
+    back = [send(crossed.at[:, own], crossed.at[:, own], back_sem, (0,), g.sibling())]
     for q in (0, 1):
         for copy in far[q]:
             copy.wait_recv()
@@ -242,20 +258,21 @@
         copy.wait()
 
 
-def gram_sum(nx, ny, nz, gram, cross):
-    rows, depth = gram.shape[1], cross.shape[1]
+def gram_sum(nx, ny, nz, gram, momentum, power):
+    rows, depth = gram.shape[0], momentum.shape[1]
     return pl.pallas_call(
         functools.partial(gram_kernel, nx, ny, nz),
         name="gram_sum",
         out_shape=(
             jax.ShapeDtypeStruct((4, nx, ny, rows, HALF // 2), F32),
-            jax.ShapeDtypeStruct((2, depth, HALF), F32),
+            jax.ShapeDtypeStruct((depth, RANK), F32),
         ),
-        in_specs=[pl.BlockSpec(memory_space=VMEM)] * 2,
+        in_specs=[pl.BlockSpec(memory_space=VMEM)] * 3,
         out_specs=(pl.BlockSpec(memory_space=VMEM),) * 2,
         scratch_shapes=[
             VMEM((rows, HALF), F32),
             VMEM((nz, rows, HALF), F32),
+            VMEM((depth, RANK), F32),
             VMEM((depth, HALF), F32),
             VMEM((depth, HALF), F32),
             VMEM((nz - 1, depth // nz, HALF), F32),
@@ -265,7 +282,7 @@
             pltpu.SemaphoreType.DMA((2, 3)),
         ],
         compiler_params=pltpu.CompilerParams(collective_id=1, has_side_effects=True),
-    )(gram, cross)
+    )(gram, momentum, power)
 
 
 def norm_kernel(nx, ny, nz, part, out, recv, total, sems):
@@ -306,7 +323,7 @@
             pltpu.SemaphoreType.DMA((2, 2, nx - 1)),
         ],
         compiler_params=pltpu.CompilerParams(collective_id=2, has_side_effects=True),
-    )(jnp.broadcast_to(part, (2, 1, RANK)))
+    )(part)
 
 
 def dot(a, b, ca, cb):
@@ -315,11 +332,108 @@
     )
 
 
-def inverse_factor(gram):
-    chol = jnp.linalg.cholesky(gram, symmetrize_input=False)
-    return lax.linalg.triangular_solve(
-        chol, jnp.eye(RANK, dtype=F32), left_side=True, lower=True
+def rowcast(x, k):
+    return jnp.broadcast_to(x[k : k + 1, :], (8, BLOCK))
+
+
+def factor_block(a, x):
+    lane = lax.broadcasted_iota(jnp.int32, (8, BLOCK), 1)
+    sub = lax.broadcasted_iota(jnp.int32, (8, BLOCK), 0)
+    tiles = BLOCK // 8
+    for t in range(tiles):
+        x[8 * t : 8 * t + 8, :] = jnp.where(lane == sub + 8 * t, 1.0, 0.0)
+    for t in range(tiles):
+        rows = a[8 * t : 8 * t + 8, :]
+        inverse = x[8 * t : 8 * t + 8, :]
+        columns = [jnp.broadcast_to(rows[:, 8 * t + k : 8 * t + k + 1], (8, BLOCK)) for k in range(8)]
+        done = inverse
+        pivots, ahead, row_a, row_x = [], [], [], []
+        for k in range(8):
+            root = lax.rsqrt(rowcast(columns[k], k))
+            pivots.append(root)
+            row_a.append(rowcast(rows, k) * root)
+            row_x.append(rowcast(inverse, k) * root)
+            done = jnp.where(sub == k, row_x[k], done)
+            ahead.append([rowcast(columns[l], k) * root for l in range(k + 1, 8)])
+            if k == 7:
+                break
+            weight = jnp.where(sub > k, columns[k] * root, 0.0)
+            for l in range(k + 1, 8):
+                columns[l] = columns[l] - weight * ahead[k][l - k - 1]
+            rows = rows - weight * row_a[k]
+            inverse = inverse - weight * row_x[k]
+        x[8 * t : 8 * t + 8, :] = done
+        for s in range(t + 1, tiles):
+            rest = a[8 * s : 8 * s + 8, :]
+            rest_x = x[8 * s : 8 * s + 8, :]
+            columns = [
+                jnp.broadcast_to(rest[:, 8 * t + k : 8 * t + k + 1], (8, BLOCK)) for k in range(8)
+            ]
+            for k in range(8):
+                weight = columns[k] * pivots[k]
+                rest = rest - weight * row_a[k]
+                rest_x = rest_x - weight * row_x[k]
+                for l in range(k + 1, 8):
+                    columns[l] = columns[l] - weight * ahead[k][l - k - 1]
+            a[8 * s : 8 * s + 8, :] = rest
+            x[8 * s : 8 * s + 8, :] = rest_x
+
+
+def full_dot(a, b, ca, cb):
+    return lax.dot_general(
+        a, b, (((ca,), (cb,)), ((), ())), precision=lax.Precision.HIGHEST, preferred_element_type=F32
     )
+
+
+def inverse_kernel(gram, crossed, out, cross, col_sq, a, block, small):
+    a[...] = gram[...]
+    out[...] = jnp.zeros_like(out)
+
+    @pl.loop(0, RANK // BLOCK)
+    def _(step):
+        block[...] = a[step, pl.ds(pl.multiple_of(step * BLOCK, BLOCK), BLOCK), :]
+        factor_block(block, small)
+        for i in range(RANK // BLOCK):
+
+            @pl.when(step == i)
+            def _():
+                low, high = i * BLOCK, (i + 1) * BLOCK
+                diagonal = small[...]
+                out[low:high, low:high] = diagonal
+                if i:
+                    out[low:high, :low] = full_dot(diagonal, out[low:high, :low], 1, 0)
+                if high < RANK:
+                    below = full_dot(a[i, high:, :], diagonal, 1, 1)
+                    for j in range(i + 1, RANK // BLOCK):
+                        top = (j - i - 1) * BLOCK
+                        a[j, j * BLOCK :, :] -= full_dot(
+                            below[top:], below[top : top + BLOCK], 1, 1
+                        )
+                    out[high:, :high] -= full_dot(below, out[low:high, :high], 1, 0)
+
+    value = dot3(crossed[...], out[...], 1, 1)
+    cross[...] = value
+    col_sq[...] = jnp.broadcast_to(jnp.sum(value * value, axis=0, keepdims=True), (2, 1, RANK))
+
+
+def inverse_factor(gram, crossed):
+    depth = crossed.shape[0]
+    return pl.pallas_call(
+        inverse_kernel,
+        name="inverse_factor",
+        out_shape=(
+            jax.ShapeDtypeStruct((RANK, RANK), F32),
+            jax.ShapeDtypeStruct((depth, RANK), F32),
+            jax.ShapeDtypeStruct((2, 1, RANK), F32),
+        ),
+        in_specs=[pl.BlockSpec(memory_space=VMEM)] * 2,
+        out_specs=(pl.BlockSpec(memory_space=VMEM),) * 3,
+        scratch_shapes=[
+            VMEM((RANK // BLOCK, RANK, BLOCK), F32),
+            VMEM((BLOCK, BLOCK), F32),
+            VMEM((BLOCK, BLOCK), F32),
+        ],
+    )(gram, crossed)
 
 
 def body(nx, ny, nz, momentum_prev, gradient, q_prev):
@@ -327,18 +441,13 @@
     power = power_sum(nx, ny, nz, dot(momentum, q_prev, 1, 0))
     rows = RANK // (nx * ny)
     mine = lax.dynamic_slice(power, (0, rows * lax.axis_index("cols")), (power.shape[0], rows))
-    gram_part = dot(mine, power, 0, 0).reshape(rows, 2, HALF).transpose(1, 0, 2)
-    depth = momentum.shape[1]
-    cross_part = dot(momentum, power, 0, 0).reshape(depth, 2, HALF).transpose(1, 0, 2)
-    gram, crossed = gram_sum(nx, ny, nz, gram_part, cross_part)
-    gram = gram.reshape(4, RANK, RANK // 4).transpose(1, 0, 2).reshape(RANK, RANK)
-    crossed = crossed.transpose(1, 0, 2).reshape(depth, RANK)
-    inverse = inverse_factor(gram)
-    cross = dot(crossed, inverse, 1, 1)
-    col_sq = norm_sum(nx, ny, nz, jnp.sum(cross * cross, axis=0, keepdims=True))
+    gram, crossed = gram_sum(nx, ny, nz, dot(mine, power, 0, 0), momentum, power)
+    inverse, cross, col_sq = inverse_factor(gram.reshape(4, RANK, RANK // 4), crossed)
+    col_sq = norm_sum(nx, ny, nz, col_sq)
     q_next = cross / (jnp.sqrt(col_sq) + 1e-08)
     factor = D / jnp.sqrt(jnp.float32(RANK))
     both = jnp.concatenate([-0.5 * cross, factor * q_next], axis=0)
+    depth = cross.shape[0]
     product = dot(power, dot(inverse, both, 0, 1), 1, 0)
     return (
         momentum + product[:, :depth],

time: 270 us -> 135 us (0.50)
  other arithmetic: 131 us -> 4.25 us
  Pallas kernels: 100 us -> 122 us
  local copies, waits for them, and re-layouts: 18.6 us -> 1.27 us
  matrix products: 15.8 us -> 5.58 us
  between operations: 3.58 us -> 0.71 us
    another operation x17 -> x0, other arithmetic: 128 us -> none  [the longest x14 88.8 us: inverse_factor(): chol = jnp.linalg.cholesky(gram, symmetrize_input=False)]
    pallas_call x0 -> x1, Pallas kernels: none -> 21.8 us  [inverse_factor(): pl.pallas_call(inverse_kernel, name='inverse_factor', out_shape=(jax.Shap...]
    another operation x17 -> x0, local copies, waits for them, and re-layouts: 10.2 us -> none
    another operation x13 -> x0, matrix products: 7.49 us -> none  [the longest x6 4.49 us: inverse_factor(): chol = jnp.linalg.cholesky(gram, symmetrize_input=False)]
    unnamed x25 -> x10, local copies, waits for them, and re-layouts: 4.32 us -> 0.6 us
    dot_general x6 -> x4, matrix products: 8.35 us -> 5.58 us  [dot(): lax.dot_general(a, b, (((ca,), (cb,)), ((), ())), precision=HIGH, preferr...]
    reshape x2 -> x0, local copies, waits for them, and re-layouts: 2.74 us -> none  [the longest x1 1.9 us: body(): gram.reshape(4, RANK, RANK // 4).transpose(1, 0, 2).reshape(RANK, RANK)]
where the time goes in v2:
time: 135 us; the launch traced here: 134 us
  Pallas kernels  122 us (90%)
  matrix products  5.58 us (4%)
  other arithmetic  4.25 us (3%)
    pallas_call x1, Pallas kernels, gram_sum(): pl.pallas_call(functools.partial(gram_kernel, nx, ny, nz), name='gram_sum...  45.7 us
    pallas_call x1, Pallas kernels, power_sum(): pl.pallas_call(functools.partial(power_kernel, nx, ny, nz), name='power_s...  42 us
    pallas_call x1, Pallas kernels, inverse_factor(): pl.pallas_call(inverse_kernel, name='inverse_factor', out_shape=(jax.Shap...  21.8 us
    pallas_call x1, Pallas kernels, norm_sum(): pl.pallas_call(functools.partial(norm_kernel, nx, ny, nz), name='norm_sum...  12.5 us
    dot_general x4, matrix products, dot(): lax.dot_general(a, b, (((ca,), (cb,)), ((), ())), precision=HIGH, preferr...  5.58 us

profile of v2, /device:TPU:1, one launch (start us, length us, event | category | flops | bytes accessed | tf_op | source)
XLA Modules:
  0.0 133.9 jit_solution(16882745903210409438)
XLA Ops:
  0.6 0.0 copy-start
  0.7 1.1 convert_add_fusion.momentum
  1.7 0.0 copy-done
  1.7 0.0 copy-start.2
  1.8 1.6 %fusion.8.part = f32[512,512]{1,0:T(8,128)} fusion(f32[512,128]{1,0:T(8,128)S(1)} %convert_add_fusion.momentum, f32[128,512]{1,0:T(8,128)S(1)} %copy-done), kind=kOutput, calls=%fused_computation.15 | convolution fusion | flops 201326592 | bytes 1572864 | tf_op jit(solution)/shard_map/dot_general | solution.py:330
  3.4 0.0 copy-done.2
  3.4 42.0 %power_sum.1.power = f32[512,512]{1,0:T(8,128)} custom-call(f32[512,512]{1,0:T(8,128)} %fusion.8.part), custom_call_target="tpu_custom_call" | custom-call | tf_op jit(solution)/shard_map/power_sum/pallas_call | solution.py:168
  45.4 2.4 %fusion.4.gram = f32[8,512]{1,0:T(8,128)} fusion(f32[512,512]{1,0:T(8,128)} %power_sum.1.power, s32[]{:T(128)S(6)} %select_n.3), kind=kOutput, calls=%fused_computation.6 | convolution fusion | flops 12582912 | bytes 1327108 | tf_op jit(solution)/shard_map/dot_general | solution.py:330
  47.8 45.7 %gram_sum.1 = (f32[4,8,8,8,128]{4,3,2,1,0:T(8,128)}, f32[128,512]{1,0:T(8,128)}) custom-call(f32[8,512]{1,0:T(8,128)} %fusion.4.gram, f32[512,128]{1,0:T(8,128)} %copy-done.2, f32[512,512]{1,0:T(8,128)} %power_sum.1.power), custom_call_target="tpu_custom_call" | custom-call | tf_op jit(solution)/shard_map/gram_sum/pallas_call | solution.py:263
  93.5 21.8 %inverse_factor.1 = (f32[512,512]{1,0:T(8,128)}, f32[128,512]{1,0:T(8,128)}, f32[2,1,512]{2,1,0:T(1,128)}) custom-call(f32[4,512,128]{2,1,0:T(8,128)} %bitcast.8, f32[128,512]{1,0:T(8,128)} %get-tuple-element.9.crossed), custom_call_target="tpu_custom_call" | custom-call | tf_op jit(solution)/shard_map/inverse_factor/pallas_call | solution.py:421
  115.4 0.0 copy-start.4
  115.4 12.5 %norm_sum.1 = f32[1,512]{1,0:T(1,128)} custom-call(f32[2,1,512]{2,1,0:T(1,128)} %get-tuple-element.12.part), custom_call_target="tpu_custom_call" | custom-call | tf_op jit(solution)/shard_map/norm_sum/pallas_call | solution.py:314
  127.9 0.7 sqrt_add_fusion
  128.6 1.7 %broadcast_multiply_fusion = (f32[128,512]{1,0:T(8,128)S(1)}, f32[128,512]{1,0:T(8,128)}, f32[128,512]{1,0:T(8,128)S(1)}) fusion(f32[128,512]{1,0:T(8,128)} %get-tuple-element.11, f32[512]{0:T(512)S(1)} %bitcast.9), kind=kLoop, calls=%fused_computation.9 | loop fusion | flops 196608 | bytes 1050624 | tf_op jit(solution)/shard_map/mul | solution.py:449
  130.3 0.0 copy-done.4
  130.3 0.0 copy-start.1
  130.3 1.0 fusion
  131.3 0.2 copy-done.1
  131.5 0.0 copy-start.3
  131.5 0.6 fusion.9
  132.1 0.4 copy-done.3
  132.5 0.7 slice_add_fusion
  133.2 0.7 slice.13
Async XLA Ops:
  0.6 1.1 copy-start
  1.7 1.6 %copy-start.2 = (f32[512,128]{1,0:T(8,128)}, f32[512,128]{1,0:T(8,128)S(1)}, u32[]{:S(2)}) copy-start(f32[512,128]{1,0:T(8,128)S(1)} %convert_add_fusion.momentum) | copy-start | bytes 786436
  115.4 14.9 %copy-start.4 = (f32[512,512]{1,0:T(8,128)S(1)}, f32[512,512]{1,0:T(8,128)}, u32[]{:S(2)}) copy-start(f32[512,512]{1,0:T(8,128)} %get-tuple-element.10) | copy-start | bytes 3145732
  130.3 1.2 copy-start.1
  131.5 0.9 copy-start.3

commit v3 on v0

v3 whole, which is shorter than its diff:
```python
import functools

import jax
import jax.numpy as jnp
from jax import lax
from jax.experimental import pallas as pl
from jax.experimental.pallas import tpu as pltpu
from jax.sharding import PartitionSpec as P

D = 8192
RANK = 512
HALF = RANK // 2
BLOCK = 128
MESH = pl.DeviceIdType.MESH
VMEM = pltpu.VMEM
F32 = jnp.float32
FACTOR = D / RANK**0.5


def order(n):
    return sorted(range(1, n), key=lambda d: -min(d, n - d))


class Grid:
    def __init__(self, nx, ny, nz):
        self.n = (nx, ny)
        self.nz = nz
        self.r = lax.axis_index("rows")
        self.c = lax.axis_index("cols")
        self.at = (lax.div(self.c, ny), lax.rem(self.c, ny))
        self.z, self.core = lax.div(self.r, 2), lax.rem(self.r, 2)

    def along(self, axis, d):
        return lax.rem(self.at[axis] + d, self.n[axis])

    def peer(self, axis, d):
        place = [self.at[0], self.at[1]]
        place[axis] = self.along(axis, d)
        return (self.r, place[0] * self.n[1] + place[1])

    def z_along(self, d):
        return lax.rem(self.z + d, self.nz)

    def z_peer(self, d):
        return (self.z_along(d) * 2 + self.core, self.c)

    def sibling(self):
        return (self.r + 1 - 2 * self.core, self.c)

    def plane_peers(self):
        return [self.peer(a, d) for a in (0, 1) for d in range(1, self.n[a])]

    def row_peers(self):
        return [self.sibling()] + [self.z_peer(d) for d in range(1, self.nz)]


def greet(peers):
    barrier = pltpu.get_barrier_semaphore()
    for device in peers:
        pl.semaphore_signal(barrier, inc=1, device_id=device, device_id_type=MESH)
    return lambda: pl.semaphore_wait(barrier, len(peers))


def send(src, dst, sems, slot, device):
    copy = pltpu.make_async_remote_copy(
        src_ref=src,
        dst_ref=dst,
        send_sem=sems.at[(0,) + slot],
        recv_sem=sems.at[(1,) + slot],
        device_id=device,
        device_id_type=MESH,
    )
    copy.start()
    return copy


def rowcast(x, k):
    return jnp.broadcast_to(x[k : k + 1, :], (8, BLOCK))


def factor_block(a, x):
    lane = lax.broadcasted_iota(jnp.int32, (8, BLOCK), 1)
    sub = lax.broadcasted_iota(jnp.int32, (8, BLOCK), 0)
    tiles = BLOCK // 8
    for t in range(tiles):
        x[8 * t : 8 * t + 8, :] = jnp.where(lane == sub + 8 * t, 1.0, 0.0)
    for t in range(tiles):
        rows = a[8 * t : 8 * t + 8, :]
        inverse = x[8 * t : 8 * t + 8, :]
        columns = [jnp.broadcast_to(rows[:, 8 * t + k : 8 * t + k + 1], (8, BLOCK)) for k in range(8)]
        done = inverse
        pivots, ahead, row_a, row_x = [], [], [], []
        for k in range(8):
            root = lax.rsqrt(rowcast(columns[k], k))
            pivots.append(root)
            row_a.append(rowcast(rows, k) * root)
            row_x.append(rowcast(inverse, k) * root)
            done = jnp.where(sub == k, row_x[k], done)
            ahead.append([rowcast(columns[l], k) * root for l in range(k + 1, 8)])
            if k == 7:
                break
            weight = jnp.where(sub > k, columns[k] * root, 0.0)
            for l in range(k + 1, 8):
                columns[l] = columns[l] - weight * ahead[k][l - k - 1]
            rows = rows - weight * row_a[k]
            inverse = inverse - weight * row_x[k]
        x[8 * t : 8 * t + 8, :] = done
        for s in range(t + 1, tiles):
            rest = a[8 * s : 8 * s + 8, :]
            rest_x = x[8 * s : 8 * s + 8, :]
            columns = [
                jnp.broadcast_to(rest[:, 8 * t + k : 8 * t + k + 1], (8, BLOCK)) for k in range(8)
            ]
            for k in range(8):
                weight = columns[k] * pivots[k]
                rest = rest - weight * row_a[k]
                rest_x = rest_x - weight * row_x[k]
                for l in range(k + 1, 8):
                    columns[l] = columns[l] - weight * ahead[k][l - k - 1]
            a[8 * s : 8 * s + 8, :] = rest
            x[8 * s : 8 * s + 8, :] = rest_x


def full_dot(a, b, ca, cb):
    return lax.dot_general(
        a, b, (((ca,), (cb,)), ((), ())), precision=lax.Precision.HIGHEST, preferred_element_type=F32
    )


def block(i, size):
    return pl.ds(pl.multiple_of(i * size, size), size)


def arrived(copies):
    for copy in copies:
        copy.wait_recv()


def sum_power(g, part, power, recv1, sum1, recv2, gather, sems):
    rows = part.shape[0]
    big = [rows // g.n[h] for h in (0, 1)]
    small = [big[h] // g.n[1 - h] for h in (0, 1)]
    columns = [pl.ds(h * HALF, HALF) for h in (0, 1)]
    first, second, third, fourth = [[], []], [[], []], [[], []], [[], []]
    for h in (0, 1):
        for d in order(g.n[h]):
            source = part.at[block(g.along(h, d), big[h]), columns[h]]
            first[h].append(send(source, recv1.at[h, d - 1], sems, (0, h, d - 1), g.peer(h, d)))
    for h in (0, 1):
        total = part[block(g.at[h], big[h]), columns[h]]
        arrived(first[h])
        for d in range(1, g.n[h]):
            total = total + recv1[h, d - 1]
        sum1[h] = total
        for d in order(g.n[1 - h]):
            source = sum1.at[h, block(g.along(1 - h, d), small[h])]
            second[h].append(
                send(source, recv2.at[h, d - 1], sems, (1, h, d - 1), g.peer(1 - h, d))
            )
    for h in (0, 1):
        mine = block(g.at[1 - h], small[h])
        total = sum1[h, mine]
        arrived(second[h])
        for d in range(1, g.n[1 - h]):
            total = total + recv2[h, d - 1]
        gather[h, mine] = total
        place = gather.at[h, mine]
        for d in order(g.n[1 - h]):
            third[h].append(send(place, place, sems, (2, h, d - 1), g.peer(1 - h, d)))
    for h in (0, 1):
        arrived(third[h])
        mine = block(g.at[h], big[h])
        for d in order(g.n[h]):
            place = power.at[mine, columns[h]]
            fourth[h].append(send(gather.at[h], place, sems, (3, h, d - 1), g.peer(h, d)))
        power[mine, columns[h]] = gather[h]
    for h in (0, 1):
        arrived(fourth[h])
    return sum(first + second + third + fourth, [])


def factor_gram(a, out, tile, small):
    out[...] = jnp.zeros_like(out)

    @pl.loop(0, RANK // BLOCK)
    def _(step):
        tile[...] = a[step, block(step, BLOCK), :]
        factor_block(tile, small)
        for i in range(RANK // BLOCK):

            @pl.when(step == i)
            def _():
                low, high = i * BLOCK, (i + 1) * BLOCK
                diagonal = small[...]
                out[low:high, low:high] = diagonal
                if i:
                    out[low:high, :low] = full_dot(diagonal, out[low:high, :low], 1, 0)
                if high < RANK:
                    below = full_dot(a[i, high:, :], diagonal, 1, 1)
                    for j in range(i + 1, RANK // BLOCK):
                        top = (j - i - 1) * BLOCK
                        a[j, j * BLOCK :, :] -= full_dot(
                            below[top:], below[top : top + BLOCK], 1, 1
                        )
                    out[high:, :high] -= full_dot(below, out[low:high, :high], 1, 0)


def step_kernel(
    nx, ny, nz, previous, gradient, q_prev, momentum_next, q_next, update,
    momentum, part, power, recv1, sum1, recv2, gather,
    slab, gram_core, gram_z, whole, a, tile, small, inverse,
    local, cross_core, cross_sum, cross_z, crossed, cross, squares, squares_recv,
    power_sem, core_sem, z_sem, plane_sem, back_sem, norm_sem,
):
    g = Grid(nx, ny, nz)
    x, y = g.at
    core = g.core
    ready = greet(g.plane_peers() + g.row_peers())
    momentum[...] = 0.95 * previous[...] + gradient[...].astype(F32)
    part[...] = full_dot(momentum[...], q_prev[...], 1, 0)
    ready()
    sent = sum_power(g, part, power, recv1, sum1, recv2, gather, power_sem)

    rows = RANK // (nx * ny)
    share = local.shape[0] // nz
    own, other = block(core, HALF), block(1 - core, HALF)
    first = g.c * rows
    slab[...] = full_dot(power[:, block(lax.div(first, BLOCK), BLOCK)], power[...], 0, 0)
    mine = pl.ds(pl.multiple_of(lax.rem(first, BLOCK), rows), rows)
    swap = [send(slab.at[mine, other], gram_core, core_sem, (0,), g.sibling())]
    local[...] = full_dot(momentum[...], power[...], 0, 0)
    swap.append(send(local.at[:, other], cross_core, core_sem, (1,), g.sibling()))
    swap[0].wait_recv()
    gram_z[g.z] = slab[mine, own] + gram_core[...]
    ups = []
    for d in order(nz):
        ups.append(send(gram_z.at[g.z], gram_z.at[g.z], z_sem, (0, d - 1), g.z_peer(d)))
    swap[1].wait_recv()
    cross_sum[...] = local[:, own] + cross_core[...]
    shares = []
    for d in order(nz):
        source = cross_sum.at[block(g.z_along(d), share)]
        shares.append(send(source, cross_z.at[d - 1], z_sem, (1, d - 1), g.z_peer(d)))
    arrived(ups)
    total = gram_z[0]
    for i in range(1, nz):
        total = total + gram_z[i]
    near, far = [[], []], [[], []]
    for q in (0, 1):
        place = whole.at[core * 2 + q, x, y]
        whole[core * 2 + q, x, y] = total[:, q * BLOCK : (q + 1) * BLOCK]
        for d in order(g.n[1 - q]):
            near[q].append(send(place, place, plane_sem, (0, q, d - 1), g.peer(1 - q, d)))
    arrived(shares)
    mine = block(g.z, share)
    total = cross_sum[mine]
    for d in range(1, nz):
        total = total + cross_z[d - 1]
    crossed[mine, own] = total
    gathers = []
    place = crossed.at[mine, own]
    for d in order(nz):
        gathers.append(send(place, place, z_sem, (2, d - 1), g.z_peer(d)))
    for q in (0, 1):
        arrived(near[q])
        place = whole.at[core * 2 + q, x] if q == 0 else whole.at[core * 2 + q, :, y]
        for d in order(g.n[q]):
            far[q].append(send(place, place, plane_sem, (1, q, d - 1), g.peer(q, d)))
    arrived(gathers)
    place = crossed.at[:, own]
    back = [send(place, place, back_sem, (0,), g.sibling())]
    for q in (0, 1):
        arrived(far[q])
        place = whole.at[core * 2 + q]
        back.append(send(place, place, back_sem, (1 + q,), g.sibling()))
    arrived(back[1:])

    a[...] = whole[...].reshape(a.shape)
    factor_gram(a, inverse, tile, small)
    arrived(back[:1])

    cross[...] = full_dot(crossed[...], inverse[...], 1, 1)
    squares[0] = jnp.sum(cross[...] * cross[...], axis=0, keepdims=True)
    norms = [[], []]
    for axis in (0, 1):
        for d in order(g.n[axis]):
            place = squares_recv.at[axis, d - 1]
            norms[axis].append(
                send(squares.at[axis], place, norm_sem, (axis, d - 1), g.peer(axis, d))
            )
        if axis == 0:
            turned = full_dot(inverse[...], -0.5 * cross[...], 0, 1)
            momentum_next[...] = momentum[...] + full_dot(power[...], turned, 1, 0)
        arrived(norms[axis])
        total = squares[axis]
        for d in range(1, g.n[axis]):
            total = total + squares_recv[axis, d - 1]
        if axis == 0:
            squares[1] = total
    value = cross[...] / (jnp.sqrt(total) + 1e-08)
    q_next[...] = value
    turned = full_dot(inverse[...], FACTOR * value, 0, 1)
    update[...] = full_dot(power[...], turned, 1, 0).astype(update.dtype)
    for copy in sent + swap + ups + shares + gathers + near[0] + near[1] + far[0] + far[1] + back:
        copy.wait_send()
    for copy in norms[0] + norms[1]:
        copy.wait_send()


def body(nx, ny, nz, previous, gradient, q_prev):
    height, depth = previous.shape
    rows = RANK // (nx * ny)
    big, small = height // nx, height // (nx * ny)
    dma = pltpu.SemaphoreType.DMA
    return pl.pallas_call(
        functools.partial(step_kernel, nx, ny, nz),
        name="power_step",
        out_shape=(
            jax.ShapeDtypeStruct((height, depth), F32),
            jax.ShapeDtypeStruct((depth, RANK), F32),
            jax.ShapeDtypeStruct((height, depth), jnp.bfloat16),
        ),
        in_specs=[pl.BlockSpec(memory_space=VMEM)] * 3,
        out_specs=(pl.BlockSpec(memory_space=VMEM),) * 3,
        scratch_shapes=[
            VMEM((height, depth), F32),
            VMEM((height, RANK), F32),
            VMEM((height, RANK), F32),
            VMEM((2, nx - 1, big, HALF), F32),
            VMEM((2, big, HALF), F32),
            VMEM((2, ny - 1, small, HALF), F32),
            VMEM((2, big, HALF), F32),
            VMEM((BLOCK, RANK), F32),
            VMEM((rows, HALF), F32),
            VMEM((nz, rows, HALF), F32),
            VMEM((RANK // BLOCK, nx, ny, rows, BLOCK), F32),
            VMEM((RANK // BLOCK, RANK, BLOCK), F32),
            VMEM((BLOCK, BLOCK), F32),
            VMEM((BLOCK, BLOCK), F32),
            VMEM((RANK, RANK), F32),
            VMEM((depth, RANK), F32),
            VMEM((depth, HALF), F32),
            VMEM((depth, HALF), F32),
            VMEM((nz - 1, depth // nz, HALF), F32),
            VMEM((depth, RANK), F32),
            VMEM((depth, RANK), F32),
            VMEM((2, 1, RANK), F32),
            VMEM((2, nx - 1, 1, RANK), F32),
            dma((2, 4, 2, nx - 1)),
            dma((2, 2)),
            dma((2, 3, nz - 1)),
            dma((2, 2, 2, nx - 1)),
            dma((2, 3)),
            dma((2, 2, nx - 1)),
        ],
        compiler_params=pltpu.CompilerParams(
            collective_id=0, has_side_effects=True, vmem_limit_bytes=60 << 20
        ),
    )(previous, gradient, q_prev)


def sizes(mesh):
    side = {64: 8, 16: 4, 4: 2}[mesh.shape["cols"]]
    return side, side, mesh.shape["rows"] // 2


def solution(mesh):
    in_specs = (P("rows", "cols"), P("rows", "cols"), P("cols", None))
    out_specs = (P("rows", "cols"), P("cols", None), P("rows", "cols"))
    return jax.shard_map(
        functools.partial(body, *sizes(mesh)),
        mesh=mesh,
        in_specs=in_specs,
        out_specs=out_specs,
        check_vma=False,
    )
```

time: 990 us -> 118 us (0.12)
  the two profiles are of different devices: /device:TPU:8 before, /device:TPU:1 now
where the time goes in v3:
time: 118 us
  Pallas kernels  114 us (97%)
  local copies, waits for them, and re-layouts  3.37 us (3%)
    pallas_call x1, Pallas kernels, body(): pl.pallas_call(functools.partial(step_kernel, nx, ny, nz), name='power_st...  114 us
    unnamed x7, local copies, waits for them, and re-layouts  3.37 us

profile of v3, /device:TPU:1, one launch (start us, length us, event | category | flops | bytes accessed | tf_op | source)
XLA Modules:
  0.0 117.9 jit_solution(2316196434698458601)
XLA Ops:
  0.6 113.9 %power_step.1 = (f32[512,128]{1,0:T(8,128)}, f32[128,512]{1,0:T(8,128)}, bf16[512,128]{1,0:T(8,128)(2,1)}) custom-call(f32[512,128]{1,0:T(8,128)} %previous.1, bf16[512,128]{1,0:T(8,128)(2,1)} %gradient.1, f32[128,512]{1,0:T(8,128)} %q_prev.1), custom_call_target="tpu_custom_call" | custom-call | tf_op jit(solution)/shard_map/power_step/pallas_call | solution.py:315
  114.5 0.0 copy-start
  114.5 1.7 %copy.9 = f32[512,128]{1,0:T(8,128)} copy(f32[512,128]{1,0:T(8,128)} %get-tuple-element.6) | data formatting | bytes 524288
  116.2 0.0 copy-done
  116.2 0.0 copy-start.1
  116.2 0.7 copy.10
  116.9 0.3 copy-done.1
  117.2 0.7 copy.11
Async XLA Ops:
  114.5 1.7 %copy-start = (f32[128,512]{1,0:T(8,128)S(1)}, f32[128,512]{1,0:T(8,128)}, u32[]{:S(2)}) copy-start(f32[128,512]{1,0:T(8,128)} %get-tuple-element.7) | copy-start | bytes 786436
  116.2 1.0 copy-start.1

commit v4 on v3

v4 whole, which is shorter than its diff:
```python
import functools

import jax
import jax.numpy as jnp
from jax import lax
from jax.experimental import pallas as pl
from jax.experimental.pallas import tpu as pltpu
from jax.sharding import PartitionSpec as P

D = 8192
RANK = 512
HALF = RANK // 2
BLOCK = 128
MESH = pl.DeviceIdType.MESH
VMEM = pltpu.VMEM
F32 = jnp.float32
FACTOR = D / RANK**0.5


def order(n):
    return sorted(range(1, n), key=lambda d: -min(d, n - d))


class Grid:
    def __init__(self, nx, ny, nz):
        self.n = (nx, ny)
        self.nz = nz
        self.r = lax.axis_index("rows")
        self.c = lax.axis_index("cols")
        self.at = (lax.div(self.c, ny), lax.rem(self.c, ny))
        self.z, self.core = lax.div(self.r, 2), lax.rem(self.r, 2)

    def along(self, axis, d):
        return lax.rem(self.at[axis] + d, self.n[axis])

    def peer(self, axis, d):
        place = [self.at[0], self.at[1]]
        place[axis] = self.along(axis, d)
        return (self.r, place[0] * self.n[1] + place[1])

    def z_along(self, d):
        return lax.rem(self.z + d, self.nz)

    def z_peer(self, d):
        return (self.z_along(d) * 2 + self.core, self.c)

    def sibling(self):
        return (self.r + 1 - 2 * self.core, self.c)

    def cross_peer(self, d, swap):
        core = self.core + swap * (1 - 2 * self.core)
        return (2 * self.z + core, self.along(0, d) * self.n[1] + self.at[1])

    def plane_peers(self):
        return [self.peer(a, d) for a in (0, 1) for d in range(1, self.n[a])]

    def row_peers(self):
        near = [self.z_peer(d) for d in range(1, self.nz)]
        return near + [self.cross_peer(d, 1) for d in range(self.n[0])]


def greet(peers):
    barrier = pltpu.get_barrier_semaphore()
    for device in peers:
        pl.semaphore_signal(barrier, inc=1, device_id=device, device_id_type=MESH)
    return lambda: pl.semaphore_wait(barrier, len(peers))


def send(src, dst, sems, slot, device):
    copy = remote(src, dst, sems, slot, device)
    copy.start()
    return copy


def remote(src, dst, sems, slot, device):
    return pltpu.make_async_remote_copy(
        src_ref=src,
        dst_ref=dst,
        send_sem=sems.at[(0,) + slot],
        recv_sem=sems.at[(1,) + slot],
        device_id=device,
        device_id_type=MESH,
    )


def rowcast(x, k):
    return jnp.broadcast_to(x[k : k + 1, :], (8, BLOCK))


def factor_block(a, x):
    lane = lax.broadcasted_iota(jnp.int32, (8, BLOCK), 1)
    sub = lax.broadcasted_iota(jnp.int32, (8, BLOCK), 0)
    tiles = BLOCK // 8

    def tile(i):
        return slice(8 * i, 8 * i + 8)

    def splats(value, i):
        return [jnp.broadcast_to(value[:, 8 * i + k : 8 * i + k + 1], (8, BLOCK)) for k in range(8)]

    rows = a[tile(0), :]
    columns = splats(rows, 0)
    for t in range(tiles):
        panel = (lane >= 8 * t) & (lane < 8 * t + 8)
        rows = jnp.where(panel, jnp.where(lane == sub + 8 * t, 1.0, 0.0), rows)
        roots, ahead, scaled = [], [], []
        for k in range(8):
            root = lax.rsqrt(rowcast(columns[k], k))
            roots.append(root)
            scaled.append(rowcast(rows, k) * root)
            ahead.append([rowcast(columns[l], k) * root for l in range(k + 1, 8)])
            if k == 7:
                break
            weight = jnp.where(sub > k, columns[k] * root, 0.0)
            for l in range(k + 1, 8):
                columns[l] = columns[l] - weight * ahead[k][l - k - 1]
            rows = rows - weight * scaled[k]
        done = scaled[0]
        for k in range(1, 8):
            done = jnp.where(sub == k, scaled[k], done)
        x[tile(t), :] = jnp.where(lane < 8 * t + 8, done, 0.0)
        for s in range(t + 1, tiles):
            rest = a[tile(s), :]
            below = splats(rest, t)
            following = splats(rest, t + 1) if s == t + 1 else []
            rest = jnp.where(panel, 0.0, rest)
            for k in range(8):
                weight = below[k] * roots[k]
                rest = rest - weight * scaled[k]
                for l in range(k + 1, 8):
                    below[l] = below[l] - weight * ahead[k][l - k - 1]
                if following:
                    following = [v - weight * rowcast(weight, l) for l, v in enumerate(following)]
            if s == t + 1:
                rows, columns = rest, following
            else:
                a[tile(s), :] = rest


def full_dot(a, b, ca, cb):
    return lax.dot_general(
        a, b, (((ca,), (cb,)), ((), ())), precision=lax.Precision.HIGHEST, preferred_element_type=F32
    )


def block(i, size):
    return pl.ds(pl.multiple_of(i * size, size), size)


def arrived(copies):
    for copy in copies:
        copy.wait_recv()


def scatter_power(g, part, rows, recv1, sum1, recv2, sems):
    columns = [pl.ds(h * HALF, HALF) for h in (0, 1)]
    first, second = [[], []], [[], []]

    def strip(h, i):
        return part.at[i, :, :, columns[0]] if h == 0 else part.at[:, i, :, columns[1]]

    for h in (0, 1):
        for d in order(g.n[h]):
            source = strip(h, g.along(h, d))
            first[h].append(send(source, recv1.at[h, d - 1], sems, (0, h, d - 1), g.peer(h, d)))
    for h in (0, 1):
        total = strip(h, g.at[h])[...]
        arrived(first[h])
        for d in range(1, g.n[h]):
            total = total + recv1[h, d - 1]
        sum1[h] = total
        for d in order(g.n[1 - h]):
            source = sum1.at[h, g.along(1 - h, d)]
            second[h].append(
                send(source, recv2.at[h, d - 1], sems, (1, h, d - 1), g.peer(1 - h, d))
            )
    for h in (0, 1):
        total = sum1[h, g.at[1 - h]]
        arrived(second[h])
        for d in range(1, g.n[1 - h]):
            total = total + recv2[h, d - 1]
        rows[:, columns[h]] = total
    return sum(first + second, [])


def factor_gram(a, out, tile, small, between):
    out[...] = jnp.zeros_like(out)

    @pl.loop(0, RANK // BLOCK)
    def _(step):
        tile[...] = a[step, block(step, BLOCK), :]
        factor_block(tile, small)
        for i in range(RANK // BLOCK):

            @pl.when(step == i)
            def _():
                if i < len(between):
                    between[i]()
                low, high = i * BLOCK, (i + 1) * BLOCK
                diagonal = small[...]
                out[low:high, low:high] = diagonal
                if i:
                    out[low:high, :low] = full_dot(diagonal, out[low:high, :low], 1, 0)
                if high < RANK:
                    below = full_dot(a[i, high:, :], diagonal, 1, 1)
                    for j in range(i + 1, RANK // BLOCK):
                        top = (j - i - 1) * BLOCK
                        a[j, j * BLOCK :, :] -= full_dot(
                            below[top:], below[top : top + BLOCK], 1, 1
                        )
                    out[high:, :high] -= full_dot(below, out[low:high, :high], 1, 0)


def step_kernel(
    nx, ny, nz, previous, gradient, q_prev, momentum_next, q_next, update,
    momentum, part, power, recv1, sum1, recv2, near_y, near_x,
    slab, gram_recv, gram_z, whole, a, tile, small, inverse,
    local, cross_core, cross_sum, cross_z, crossed, cross, squares, squares_recv,
    power_sem, near_sem, bulk_sem, gram_sem, core_sem, z_sem, plane_sem, back_sem, norm_sem,
):
    g = Grid(nx, ny, nz)
    x, y = g.at
    core = g.core
    ready = greet(g.plane_peers() + g.row_peers())
    momentum[...] = 0.95 * previous[...] + gradient[...].astype(F32)
    part[...] = full_dot(momentum[...], q_prev[...], 1, 0).reshape(part.shape)
    ready()
    sent = scatter_power(g, part, near_y.at[y], recv1, sum1, recv2, power_sem)

    halves = [pl.ds(h * HALF, HALF) for h in (0, 1)]
    near_x[x] = near_y[y, :, HALF:]
    strips = [[], []]
    for d in order(ny):
        place = near_y.at[y]
        strips[0].append(send(place, place, near_sem, (0, d - 1), g.peer(1, d)))
    for d in order(nx):
        place = near_x.at[x]
        strips[1].append(send(place, place, near_sem, (1, d - 1), g.peer(0, d)))
    arrived(strips[0])

    rows = RANK // (nx * ny)
    group, width = RANK // ny, slab.shape[0]
    own, other = block(core, HALF), block(1 - core, HALF)
    seen = near_y[...].reshape(-1, RANK)
    near_y_part = near_y[:, :, block(lax.div(y * group, width), width)].reshape(-1, width)
    slab[...] = full_dot(near_y_part, seen, 0, 0)
    start = lax.rem(y * group, width)

    def piece(i):
        return pl.ds(pl.multiple_of(start + i * rows, rows), rows)

    spread = []
    for d in order(nx) + [0]:
        for swap in (0, 1):
            if d or swap:
                source = slab.at[piece(g.along(0, d)), other if swap else own]
                slot = 2 * d + swap - 1
                spread.append(
                    send(source, gram_recv.at[slot], gram_sem, (slot,), g.cross_peer(d, swap))
                )

    bulk = [[], []]
    power[x, :, :, halves[0]] = near_y[:, :, :HALF]
    for d in order(nx):
        place = power.at[x, :, :, halves[0]]
        bulk[0].append(
            send(near_y.at[:, :, halves[0]], place, bulk_sem, (0, d - 1), g.peer(0, d))
        )
    arrived(strips[1])
    power[:, y, :, halves[1]] = near_x[...]
    for d in order(ny):
        place = power.at[:, y, :, halves[1]]
        bulk[1].append(send(near_x, place, bulk_sem, (1, d - 1), g.peer(1, d)))

    total = slab[piece(x), own]
    arrived(spread)
    for slot in range(2 * nx - 1):
        total = total + gram_recv[slot]
    gram_z[g.z] = total
    ups = []
    for d in order(nz):
        ups.append(send(gram_z.at[g.z], gram_z.at[g.z], z_sem, (0, d - 1), g.z_peer(d)))
    arrived(ups)
    total = gram_z[0]
    for i in range(1, nz):
        total = total + gram_z[i]
    near, far, back = [[], []], [[], []], [[], []]
    for q in (0, 1):
        place = whole.at[core * 2 + q, y, x]
        whole[core * 2 + q, y, x] = total[:, q * BLOCK : (q + 1) * BLOCK]
        for d in order(g.n[q]):
            near[q].append(send(place, place, plane_sem, (0, q, d - 1), g.peer(q, d)))

    arrived(bulk[0] + bulk[1])
    share = local.shape[0] // nz
    local[...] = full_dot(momentum[...], power[...].reshape(-1, RANK), 0, 0)
    swapped = send(local.at[:, other], cross_core, core_sem, (0,), g.sibling())

    def line(q, i):
        return whole.at[core * 2, i] if q == 0 else whole.at[core * 2 + 1, :, i]

    for q in (0, 1):
        arrived(near[q])
        place = line(q, g.at[1 - q])
        for d in order(g.n[1 - q]):
            far[q].append(send(place, place, plane_sem, (1, q, d - 1), g.peer(1 - q, d)))
        back[q].append(send(place, place, back_sem, (q, 0), g.sibling()))
    swapped.wait_recv()
    cross_sum[...] = local[:, own] + cross_core[...]
    shares = []
    for d in order(nz):
        source = cross_sum.at[block(g.z_along(d), share)]
        shares.append(send(source, cross_z.at[d - 1], z_sem, (1, d - 1), g.z_peer(d)))
    for i in range(nx - 1):
        for q in (0, 1):
            far[q][i].wait_recv()
            d = order(nx)[i]
            place = line(q, g.along(1 - q, g.n[1 - q] - d))
            back[q].append(send(place, place, back_sem, (q, d), g.sibling()))
    arrived(back[0] + back[1])

    mine = block(g.z, share)

    def sum_shares():
        arrived(shares)
        total = cross_sum[mine]
        for d in range(1, nz):
            total = total + cross_z[d - 1]
        crossed[mine, own] = total
        place = crossed.at[mine, own]
        for d in order(nz):
            send(place, place, z_sem, (2, d - 1), g.z_peer(d))

    def gathers():
        place = crossed.at[mine, own]
        return [remote(place, place, z_sem, (2, d - 1), g.z_peer(d)) for d in order(nz)]

    def last():
        place = crossed.at[:, own]
        return remote(place, place, core_sem, (1,), g.sibling())

    def share_sums():
        arrived(gathers())
        last().start()

    a[...] = whole[...].reshape(a.shape)
    factor_gram(a, inverse, tile, small, [sum_shares, share_sums])
    last().wait_recv()

    cross[...] = full_dot(crossed[...], inverse[...], 1, 1)
    squares[0] = jnp.sum(cross[...] * cross[...], axis=0, keepdims=True)
    norms = [[], []]
    for axis in (0, 1):
        for d in order(g.n[axis]):
            place = squares_recv.at[axis, d - 1]
            norms[axis].append(
                send(squares.at[axis], place, norm_sem, (axis, d - 1), g.peer(axis, d))
            )
        if axis == 0:
            turned = full_dot(inverse[...], -0.5 * cross[...], 0, 1)
            momentum_next[...] = momentum[...] + full_dot(
                power[...].reshape(-1, RANK), turned, 1, 0
            )
        arrived(norms[axis])
        total = squares[axis]
        for d in range(1, g.n[axis]):
            total = total + squares_recv[axis, d - 1]
        if axis == 0:
            squares[1] = total
    value = cross[...] / (jnp.sqrt(total) + 1e-08)
    q_next[...] = value
    turned = full_dot(inverse[...], FACTOR * value, 0, 1)
    update[...] = full_dot(power[...].reshape(-1, RANK), turned, 1, 0).astype(update.dtype)
    groups = [sent, spread, ups, shares, gathers(), [swapped, last()]]
    for copy in sum(groups + strips + bulk + near + far + back + norms, []):
        copy.wait_send()


def body(nx, ny, nz, previous, gradient, q_prev):
    height, depth = previous.shape
    rows = RANK // (nx * ny)
    small = height // (nx * ny)
    dma = pltpu.SemaphoreType.DMA
    return pl.pallas_call(
        functools.partial(step_kernel, nx, ny, nz),
        name="power_step",
        out_shape=(
            jax.ShapeDtypeStruct((height, depth), F32),
            jax.ShapeDtypeStruct((depth, RANK), F32),
            jax.ShapeDtypeStruct((height, depth), jnp.bfloat16),
        ),
        in_specs=[pl.BlockSpec(memory_space=VMEM)] * 3,
        out_specs=(pl.BlockSpec(memory_space=VMEM),) * 3,
        scratch_shapes=[
            VMEM((height, depth), F32),
            VMEM((nx, ny, small, RANK), F32),
            VMEM((nx, ny, small, RANK), F32),
            VMEM((2, nx - 1, ny, small, HALF), F32),
            VMEM((2, ny, small, HALF), F32),
            VMEM((2, ny - 1, small, HALF), F32),
            VMEM((ny, small, RANK), F32),
            VMEM((nx, small, HALF), F32),
            VMEM((max(BLOCK, RANK // ny), RANK), F32),
            VMEM((2 * nx - 1, rows, HALF), F32),
            VMEM((nz, rows, HALF), F32),
            VMEM((RANK // BLOCK, ny, nx, rows, BLOCK), F32),
            VMEM((RANK // BLOCK, RANK, BLOCK), F32),
            VMEM((BLOCK, BLOCK), F32),
            VMEM((BLOCK, BLOCK), F32),
            VMEM((RANK, RANK), F32),
            VMEM((depth, RANK), F32),
            VMEM((depth, HALF), F32),
            VMEM((depth, HALF), F32),
            VMEM((nz - 1, depth // nz, HALF), F32),
            VMEM((depth, RANK), F32),
            VMEM((depth, RANK), F32),
            VMEM((2, 1, RANK), F32),
            VMEM((2, nx - 1, 1, RANK), F32),
            dma((2, 2, 2, nx - 1)),
            dma((2, 2, nx - 1)),
            dma((2, 2, nx - 1)),
            dma((2, 2 * nx - 1)),
            dma((2, 2)),
            dma((2, 3, nz - 1)),
            dma((2, 2, 2, nx - 1)),
            dma((2, 2, nx)),
            dma((2, 2, nx - 1)),
        ],
        compiler_params=pltpu.CompilerParams(
            collective_id=0, has_side_effects=True, vmem_limit_bytes=60 << 20
        ),
    )(previous, gradient, q_prev)


def sizes(mesh):
    side = {64: 8, 16: 4, 4: 2}[mesh.shape["cols"]]
    return side, side, mesh.shape["rows"] // 2


def solution(mesh):
    in_specs = (P("rows", "cols"), P("rows", "cols"), P("cols", None))
    out_specs = (P("rows", "cols"), P("cols", None), P("rows", "cols"))
    return jax.shard_map(
        functools.partial(body, *sizes(mesh)),
        mesh=mesh,
        in_specs=in_specs,
        out_specs=out_specs,
        check_vma=False,
    )
```

time: 118 us -> 109 us (0.924)
  Pallas kernels: 114 us -> 105 us
    pallas_call x1, Pallas kernels: 114 us -> 105 us  [body(): pl.pallas_call(functools.partial(step_kernel, nx, ny, nz), name='power_st...]
where the time goes in v4:
time: 109 us
  Pallas kernels  105 us (96%)
  local copies, waits for them, and re-layouts  3.37 us (3%)
    pallas_call x1, Pallas kernels, body(): pl.pallas_call(functools.partial(step_kernel, nx, ny, nz), name='power_st...  105 us
    unnamed x7, local copies, waits for them, and re-layouts  3.37 us

profile of v4, /device:TPU:1, one launch (start us, length us, event | category | flops | bytes accessed | tf_op | source)
XLA Modules:
  0.0 108.7 jit_solution(12610095777459303229)
XLA Ops:
  0.6 104.7 %power_step.1 = (f32[512,128]{1,0:T(8,128)}, f32[128,512]{1,0:T(8,128)}, bf16[512,128]{1,0:T(8,128)(2,1)}) custom-call(f32[512,128]{1,0:T(8,128)} %previous.1, bf16[512,128]{1,0:T(8,128)(2,1)} %gradient.1, f32[128,512]{1,0:T(8,128)} %q_prev.1), custom_call_target="tpu_custom_call" | custom-call | tf_op jit(solution)/shard_map/power_step/pallas_call | solution.py:384
  105.3 0.0 copy-start
  105.3 1.7 %copy.9 = f32[512,128]{1,0:T(8,128)} copy(f32[512,128]{1,0:T(8,128)} %get-tuple-element.6) | data formatting | bytes 524288
  107.0 0.0 copy-done
  107.0 0.0 copy-start.1
  107.0 0.7 copy.10
  107.7 0.3 copy-done.1
  108.0 0.7 copy.11
Async XLA Ops:
  105.3 1.7 %copy-start = (f32[128,512]{1,0:T(8,128)S(1)}, f32[128,512]{1,0:T(8,128)}, u32[]{:S(2)}) copy-start(f32[128,512]{1,0:T(8,128)} %get-tuple-element.7) | copy-start | bytes 786436
  107.0 1.0 copy-start.1

commit v5 on v4

--- a/solution.py
+++ b/solution.py
@@ -212,17 +212,16 @@
 
 
 def step_kernel(
-    nx, ny, nz, previous, gradient, q_prev, momentum_next, q_next, update,
-    momentum, part, power, recv1, sum1, recv2, near_y, near_x,
+    nx, ny, nz, momentum, q_prev, basis, cross, col_sq,
+    part, power, recv1, sum1, recv2, near_y, near_x,
     slab, gram_recv, gram_z, whole, a, tile, small, inverse,
-    local, cross_core, cross_sum, cross_z, crossed, cross, squares, squares_recv,
+    local, cross_core, cross_sum, cross_z, crossed, squares, squares_recv,
     power_sem, near_sem, bulk_sem, gram_sem, core_sem, z_sem, plane_sem, back_sem, norm_sem,
 ):
     g = Grid(nx, ny, nz)
     x, y = g.at
     core = g.core
     ready = greet(g.plane_peers() + g.row_peers())
-    momentum[...] = 0.95 * previous[...] + gradient[...].astype(F32)
     part[...] = full_dot(momentum[...], q_prev[...], 1, 0).reshape(part.shape)
     ready()
     sent = scatter_power(g, part, near_y.at[y], recv1, sum1, recv2, power_sem)
@@ -347,8 +346,9 @@
     factor_gram(a, inverse, tile, small, [sum_shares, share_sums])
     last().wait_recv()
 
-    cross[...] = full_dot(crossed[...], inverse[...], 1, 1)
-    squares[0] = jnp.sum(cross[...] * cross[...], axis=0, keepdims=True)
+    value = full_dot(crossed[...], inverse[...], 1, 1)
+    cross[...] = value
+    squares[0] = jnp.sum(value * value, axis=0, keepdims=True)
     norms = [[], []]
     for axis in (0, 1):
         for d in order(g.n[axis]):
@@ -357,42 +357,43 @@
                 send(squares.at[axis], place, norm_sem, (axis, d - 1), g.peer(axis, d))
             )
         if axis == 0:
-            turned = full_dot(inverse[...], -0.5 * cross[...], 0, 1)
-            momentum_next[...] = momentum[...] + full_dot(
-                power[...].reshape(-1, RANK), turned, 1, 0
-            )
+            basis[...] = full_dot(power[...].reshape(-1, RANK), inverse[...], 1, 1)
         arrived(norms[axis])
         total = squares[axis]
         for d in range(1, g.n[axis]):
             total = total + squares_recv[axis, d - 1]
         if axis == 0:
             squares[1] = total
-    value = cross[...] / (jnp.sqrt(total) + 1e-08)
-    q_next[...] = value
-    turned = full_dot(inverse[...], FACTOR * value, 0, 1)
-    update[...] = full_dot(power[...].reshape(-1, RANK), turned, 1, 0).astype(update.dtype)
+    col_sq[...] = total
     groups = [sent, spread, ups, shares, gathers(), [swapped, last()]]
     for copy in sum(groups + strips + bulk + near + far + back + norms, []):
         copy.wait_send()
 
 
+def finish_kernel(momentum, basis, cross, col_sq, momentum_next, q_next, update):
+    momentum_next[...] = momentum[...] - 0.5 * full_dot(basis[...], cross[...], 1, 1)
+    value = cross[...] / (jnp.sqrt(col_sq[...]) + 1e-08)
+    q_next[...] = value
+    update[...] = (FACTOR * full_dot(basis[...], value, 1, 1)).astype(update.dtype)
+
+
 def body(nx, ny, nz, previous, gradient, q_prev):
     height, depth = previous.shape
+    momentum = 0.95 * previous + gradient.astype(F32)
     rows = RANK // (nx * ny)
     small = height // (nx * ny)
     dma = pltpu.SemaphoreType.DMA
-    return pl.pallas_call(
+    basis, cross, col_sq = pl.pallas_call(
         functools.partial(step_kernel, nx, ny, nz),
         name="power_step",
         out_shape=(
-            jax.ShapeDtypeStruct((height, depth), F32),
+            jax.ShapeDtypeStruct((height, RANK), F32),
             jax.ShapeDtypeStruct((depth, RANK), F32),
-            jax.ShapeDtypeStruct((height, depth), jnp.bfloat16),
+            jax.ShapeDtypeStruct((1, RANK), F32),
         ),
-        in_specs=[pl.BlockSpec(memory_space=VMEM)] * 3,
+        in_specs=[pl.BlockSpec(memory_space=VMEM)] * 2,
         out_specs=(pl.BlockSpec(memory_space=VMEM),) * 3,
         scratch_shapes=[
-            VMEM((height, depth), F32),
             VMEM((nx, ny, small, RANK), F32),
             VMEM((nx, ny, small, RANK), F32),
             VMEM((2, nx - 1, ny, small, HALF), F32),
@@ -413,7 +414,6 @@
             VMEM((depth, HALF), F32),
             VMEM((nz - 1, depth // nz, HALF), F32),
             VMEM((depth, RANK), F32),
-            VMEM((depth, RANK), F32),
             VMEM((2, 1, RANK), F32),
             VMEM((2, nx - 1, 1, RANK), F32),
             dma((2, 2, 2, nx - 1)),
@@ -427,9 +427,21 @@
             dma((2, 2, nx - 1)),
         ],
         compiler_params=pltpu.CompilerParams(
-            collective_id=0, has_side_effects=True, vmem_limit_bytes=60 << 20
+            collective_id=0, has_side_effects=True, vmem_limit_bytes=40 << 20
         ),
-    )(previous, gradient, q_prev)
+    )(momentum, q_prev)
+    return pl.pallas_call(
+        finish_kernel,
+        name="finish",
+        out_shape=(
+            jax.ShapeDtypeStruct((height, depth), F32),
+            jax.ShapeDtypeStruct((depth, RANK), F32),
+            jax.ShapeDtypeStruct((height, depth), jnp.bfloat16),
+        ),
+        in_specs=[pl.BlockSpec(memory_space=VMEM)] * 4,
+        out_specs=(pl.BlockSpec(memory_space=VMEM),) * 3,
+        compiler_params=pltpu.CompilerParams(vmem_limit_bytes=24 << 20),
+    )(momentum, basis, cross, col_sq)
 
 
 def sizes(mesh):

time: 109 us -> 105 us (0.963)
  local copies, waits for them, and re-layouts: 3.37 us -> 0.01 us
  Pallas kernels: 105 us -> 102 us
    pallas_call x1, Pallas kernels: 105 us -> 99.8 us  [body(): pl.pallas_call(functools.partial(step_kernel, nx, ny, nz), name='power_st...]
    unnamed x7 -> x2, local copies, waits for them, and re-layouts: 3.37 us -> 0.01 us
    pallas_call x0 -> x1, Pallas kernels: none -> 2.52 us  [body(): pl.pallas_call(finish_kernel, name='finish', out_shape=(jax.ShapeDtypeStr...]
where the time goes in v5:
time: 105 us; the launch traced here: 104 us
  Pallas kernels  102 us (97%)
  other arithmetic  1.08 us (1%)
    pallas_call x1, Pallas kernels, body(): pl.pallas_call(functools.partial(step_kernel, nx, ny, nz), name='power_st...  99.8 us
    pallas_call x1, Pallas kernels, body(): pl.pallas_call(finish_kernel, name='finish', out_shape=(jax.ShapeDtypeStr...  2.52 us

profile of v5, /device:TPU:1, one launch (start us, length us, event | category | flops | bytes accessed | tf_op | source)
XLA Modules:
  0.0 104.1 jit_solution(5595186856711371681)
XLA Ops:
  0.6 0.0 copy-start
  0.6 1.1 %convert_add_fusion.momentum = f32[512,128]{1,0:T(8,128)S(1)} fusion(bf16[512,128]{1,0:T(8,128)(2,1)} %param.4, f32[512,128]{1,0:T(8,128)} %param.3), kind=kLoop, calls=%fused_computation | loop fusion | flops 196608 | bytes 655360 | tf_op jit(solution)/shard_map/add | solution.py:382
  1.7 0.0 copy-done
  1.7 99.8 %power_step.1 = (f32[512,512]{1,0:T(8,128)S(1)}, f32[128,512]{1,0:T(8,128)S(1)}, f32[1,512]{1,0:T(1,128)S(1)}) custom-call(f32[512,128]{1,0:T(8,128)S(1)} %convert_add_fusion.momentum, f32[128,512]{1,0:T(8,128)S(1)} %copy-done), custom_call_target="tpu_custom_call" | custom-call | tf_op jit(solution)/shard_map/power_step/pallas_call | solution.py:386
  101.5 2.5 %finish.1 = (f32[512,128]{1,0:T(8,128)}, f32[128,512]{1,0:T(8,128)}, bf16[512,128]{1,0:T(8,128)(2,1)}) custom-call(f32[512,128]{1,0:T(8,128)S(1)} %convert_add_fusion.momentum, f32[512,512]{1,0:T(8,128)S(1)} %get-tuple-element.6.basis, f32[128,512]{1,0:T(8,128)S(1)} %get-tuple-element.7.cross, f32[1,512]{1,0:T(1,128)S(1)} %get-tuple-element.8.col_sq), custom_call_target="tpu_custom_call" | custom-call | tf_op jit(solution)/shard_map/finish/pallas_call | solution.py:433
Async XLA Ops:
  0.6 1.1 %copy-start = (f32[128,512]{1,0:T(8,128)S(1)}, f32[128,512]{1,0:T(8,128)}, u32[]{:S(2)}) copy-start(f32[128,512]{1,0:T(8,128)} %q_prev.1) | copy-start | bytes 786436

commit v6 on v5

--- a/solution.py
+++ b/solution.py
@@ -152,22 +152,37 @@
         copy.wait_recv()
 
 
-def scatter_power(g, part, rows, recv1, sum1, recv2, sems):
+def scatter_power(g, part, rows, recv1, relayed, sum1, recv2, sems):
     columns = [pl.ds(h * HALF, HALF) for h in (0, 1)]
     first, second = [[], []], [[], []]
 
     def strip(h, i):
         return part.at[i, :, :, columns[0]] if h == 0 else part.at[:, i, :, columns[1]]
 
+    relays = [[], []]
     for h in (0, 1):
-        for d in order(g.n[h]):
-            source = strip(h, g.along(h, d))
+        n = g.n[h]
+        half = n // 2 if n >= 4 else n
+        if half < n:
+            source = strip(h, g.along(h, half))
+            relays[h].append(send(source, relayed.at[0, h], sems, (2, h, 0), g.peer(h, n - 1)))
+        for d in order(n):
+            if d not in (half, half + 1):
+                source = strip(h, g.along(h, d))
+                first[h].append(send(source, recv1.at[h, d - 1], sems, (0, h, d - 1), g.peer(h, d)))
+    for h in (0, 1):
+        arrived(relays[h])
+        if relays[h]:
+            d = g.n[h] // 2 + 1
+            relayed[1, h] = strip(h, g.along(h, d))[...] + relayed[0, h]
+            source = relayed.at[1, h]
             first[h].append(send(source, recv1.at[h, d - 1], sems, (0, h, d - 1), g.peer(h, d)))
     for h in (0, 1):
         total = strip(h, g.at[h])[...]
         arrived(first[h])
         for d in range(1, g.n[h]):
-            total = total + recv1[h, d - 1]
+            if not relays[h] or d != g.n[h] // 2:
+                total = total + recv1[h, d - 1]
         sum1[h] = total
         for d in order(g.n[1 - h]):
             source = sum1.at[h, g.along(1 - h, d)]
@@ -180,7 +195,7 @@
         for d in range(1, g.n[1 - h]):
             total = total + recv2[h, d - 1]
         rows[:, columns[h]] = total
-    return sum(first + second, [])
+    return sum(first + second + relays, [])
 
 
 def factor_gram(a, out, tile, small, between):
@@ -213,7 +228,7 @@
 
 def step_kernel(
     nx, ny, nz, momentum, q_prev, basis, cross, col_sq,
-    part, power, recv1, sum1, recv2, near_y, near_x,
+    part, power, recv1, relayed, sum1, recv2, near_y, near_x,
     slab, gram_recv, gram_z, whole, a, tile, small, inverse,
     local, cross_core, cross_sum, cross_z, crossed, squares, squares_recv,
     power_sem, near_sem, bulk_sem, gram_sem, core_sem, z_sem, plane_sem, back_sem, norm_sem,
@@ -224,7 +239,7 @@
     ready = greet(g.plane_peers() + g.row_peers())
     part[...] = full_dot(momentum[...], q_prev[...], 1, 0).reshape(part.shape)
     ready()
-    sent = scatter_power(g, part, near_y.at[y], recv1, sum1, recv2, power_sem)
+    sent = scatter_power(g, part, near_y.at[y], recv1, relayed, sum1, recv2, power_sem)
 
     halves = [pl.ds(h * HALF, HALF) for h in (0, 1)]
     near_x[x] = near_y[y, :, HALF:]
@@ -397,6 +412,7 @@
             VMEM((nx, ny, small, RANK), F32),
             VMEM((nx, ny, small, RANK), F32),
             VMEM((2, nx - 1, ny, small, HALF), F32),
+            VMEM((2, 2, ny, small, HALF), F32),
             VMEM((2, ny, small, HALF), F32),
             VMEM((2, ny - 1, small, HALF), F32),
             VMEM((ny, small, RANK), F32),
@@ -416,7 +432,7 @@
             VMEM((depth, RANK), F32),
             VMEM((2, 1, RANK), F32),
             VMEM((2, nx - 1, 1, RANK), F32),
-            dma((2, 2, 2, nx - 1)),
+            dma((2, 3, 2, nx - 1)),
             dma((2, 2, nx - 1)),
             dma((2, 2, nx - 1)),
             dma((2, 2 * nx - 1)),

time: 105 us -> 103 us (0.981)
    pallas_call x1, Pallas kernels: 99.8 us -> 98.7 us  [body(): pl.pallas_call(functools.partial(step_kernel, nx, ny, nz), name='power_st...]
where the time goes in v6:
time: 103 us
  Pallas kernels  101 us (98%)
  other arithmetic  1.08 us (1%)
    pallas_call x1, Pallas kernels, body(): pl.pallas_call(functools.partial(step_kernel, nx, ny, nz), name='power_st...  98.7 us
    pallas_call x1, Pallas kernels, body(): pl.pallas_call(finish_kernel, name='finish', out_shape=(jax.ShapeDtypeStr...  2.52 us

profile of v6, /device:TPU:1, one launch (start us, length us, event | category | flops | bytes accessed | tf_op | source)
XLA Modules:
  0.0 103.0 jit_solution(15191264276875205158)
XLA Ops:
  0.6 0.0 copy-start
  0.6 1.1 %convert_add_fusion.momentum = f32[512,128]{1,0:T(8,128)S(1)} fusion(bf16[512,128]{1,0:T(8,128)(2,1)} %param.4, f32[512,128]{1,0:T(8,128)} %param.3), kind=kLoop, calls=%fused_computation | loop fusion | flops 196608 | bytes 655360 | tf_op jit(solution)/shard_map/add | solution.py:397
  1.7 0.0 copy-done
  1.7 98.7 %power_step.1 = (f32[512,512]{1,0:T(8,128)S(1)}, f32[128,512]{1,0:T(8,128)S(1)}, f32[1,512]{1,0:T(1,128)S(1)}) custom-call(f32[512,128]{1,0:T(8,128)S(1)} %convert_add_fusion.momentum, f32[128,512]{1,0:T(8,128)S(1)} %copy-done), custom_call_target="tpu_custom_call" | custom-call | tf_op jit(solution)/shard_map/power_step/pallas_call | solution.py:401
  100.4 2.5 %finish.1 = (f32[512,128]{1,0:T(8,128)}, f32[128,512]{1,0:T(8,128)}, bf16[512,128]{1,0:T(8,128)(2,1)}) custom-call(f32[512,128]{1,0:T(8,128)S(1)} %convert_add_fusion.momentum, f32[512,512]{1,0:T(8,128)S(1)} %get-tuple-element.6.basis, f32[128,512]{1,0:T(8,128)S(1)} %get-tuple-element.7.cross, f32[1,512]{1,0:T(1,128)S(1)} %get-tuple-element.8.col_sq), custom_call_target="tpu_custom_call" | custom-call | tf_op jit(solution)/shard_map/finish/pallas_call | solution.py:449
Async XLA Ops:
  0.6 1.1 %copy-start = (f32[128,512]{1,0:T(8,128)S(1)}, f32[128,512]{1,0:T(8,128)}, u32[]{:S(2)}) copy-start(f32[128,512]{1,0:T(8,128)} %q_prev.1) | copy-start | bytes 786436
